TPU v7x, 256 devices: a whole 4x4x8 slice. The times are simulated.
256 devices in a mesh: box: 32 (over y, x, core), term: 8 (over z).
Axes of the slice: x: 4, y: 4, z: 8, core: 2. Of those that a mesh axis runs over, the one named last changes fastest.
Arguments:
- coeffs: bfloat16 [16, 512, 256], P(None, 'box'), may hold values from -6 to 6
- operators: bfloat16 [16, 3, 16, 16], P('term'), may hold values from -1.5 to 1.5
- neighbors: int32 [512, 13], P('box'), may hold values from -1 to 511, as said below
Outputs:
- potential: float32 [16, 512, 256], P('term', 'box')
Inputs may be any that keep to these rules, and one draw needn't show every extreme that they name: `neighbors`: entry (b, k) is the index of the box at displacement k from box b, or -1 where that box is not in the level; it is never b. Among the 16 rows of one index of box, at most 2 entries name boxes of any one other index (boxes 16 * q to 16 * q + 15); each index has exactly 2 entries naming boxes of each index next to it, and one index receives exactly 2 such entries from every other index.
All inputs are finite; a program needn't handle non-finite values.
Results may differ from a plain program's by a relative error of at most 0.0018.
Values may be sent and summed in bfloat16 or wider, within the bound.
No kernel may reach another device: no remote copies, remote signals or barrier semaphores. Data moves between devices by JAX's collectives and lax.ppermute only.
A program may use at most 128 MiB of HBM per device.

v0:
```python
import jax
import jax.numpy as jnp
from jax import lax
from jax.experimental import pallas as pl
from jax.experimental.pallas import tpu as pltpu
from jax.sharding import PartitionSpec as P

CAP = 2
BIG = 0x7FFFFFFF


def iota(shape, axis):
    return lax.broadcasted_iota(jnp.int32, shape, axis)


def request_kernel(neighbors_ref, keys_ref):
    box_count, column_count = neighbors_ref.shape
    groups = keys_ref.shape[0]
    myself = lax.axis_index("box").astype(jnp.int32)
    peer = iota((groups, column_count), 0)
    column = iota((groups, column_count), 1)
    first = jnp.full((groups, column_count), BIG, jnp.int32)
    last = jnp.full((groups, column_count), -1, jnp.int32)
    for home in range(box_count):
        named = neighbors_ref[home : home + 1, :]
        owner = jnp.where(named >= 0, named >> 4, -1)
        owner = jnp.where(owner == myself, -1, owner)
        key = ((home * column_count + column) << 16) | (column << 8) | (home << 4) | (named & 15)
        member = jnp.broadcast_to(owner, peer.shape) == peer
        first = jnp.minimum(first, jnp.where(member, key, BIG))
        last = jnp.maximum(last, jnp.where(member, key, -1))
    first = jnp.min(first, axis=1, keepdims=True)
    last = jnp.max(last, axis=1, keepdims=True)
    last = jnp.where(last == first, -1, last)
    first = jnp.where(first == BIG, -1, first)
    lane = iota(keys_ref.shape, 1)
    keys_ref[...] = jnp.where(lane == 0, first, jnp.where(lane == 1, last, -1))


def pack_kernel(operators_ref, packed_ref):
    blocks = [operators_ref[16 * i : 16 * (i + 1), :] for i in range(6)]
    pad = jnp.zeros((16, 32), operators_ref.dtype)
    row = jnp.concatenate(blocks + [pad], axis=1)
    for i in range(packed_ref.shape[0]):
        packed_ref[i] = row


def expand(rows, modulo):
    lane = iota((128, 1536), 1)
    row = iota((128, 1536), 0)
    pick = ((lane >> 8) << 4) + ((lane & 15) if modulo else ((lane >> 4) & 15))
    ones = jnp.where(pick == row, 1.0, 0.0).astype(jnp.bfloat16)
    return jnp.dot(rows, ones, preferred_element_type=jnp.float32)


def image_kernel(
    packed_ref, coeffs_ref, high_ref, low_ref, outer_ref, inner_ref, left_ref, half_ref, kron_ref
):
    term = lax.axis_index("term").astype(jnp.int32)
    rows = packed_ref[...].reshape(128, 128)
    outer_ref[...] = expand(rows, False)
    inner_ref[...] = expand(rows, True)
    diagonal = (iota((16, 256), 1) & 15) == iota((16, 256), 0)
    for r in range(16):
        d, e = divmod(r, 2)
        for m in range(3):
            lanes = slice(256 * (3 * e + m), 256 * (3 * e + m + 1))
            for al in range(2):
                row = outer_ref[pl.ds(16 * d + 2 * term + al, 1), lanes]
                block = jnp.where(diagonal, jnp.broadcast_to(row, (16, 256)), 0.0)
                at = 96 * r + 32 * m + 16 * al
                left_ref[at : at + 16, :] = block.astype(jnp.bfloat16)
    half = jnp.dot(left_ref[...], coeffs_ref[...], preferred_element_type=jnp.float32)
    half = half.astype(jnp.bfloat16)
    for r in range(16):
        half_ref[:, 256 * r : 256 * (r + 1)] = half[96 * r : 96 * (r + 1), :]
    for n in range(3):
        for p in range(3):
            slot = (3 * n + p) % 2
            for r in range(16):
                d, e = divmod(r, 2)
                at = 3 * e + n
                outer = outer_ref[16 * d : 16 * (d + 1), 256 * at : 256 * (at + 1)]
                at = 3 * e + p
                inner = inner_ref[16 * d : 16 * (d + 1), 256 * at : 256 * (at + 1)]
                product = outer[:, None, :] * inner[None, :, :]
                kron_ref[slot, :, 256 * r : 256 * (r + 1)] = product.reshape(256, 256).astype(
                    jnp.bfloat16
                )
            applied = lax.dot_general(
                half_ref[...],
                kron_ref[slot],
                (((1,), (1,)), ((), ())),
                preferred_element_type=jnp.float32,
            )
            high = applied.astype(jnp.bfloat16)
            low = (applied - high.astype(jnp.float32)).astype(jnp.bfloat16)
            for m in range(3):
                code = 9 * m + 3 * n + p
                for al in range(2):
                    at = 32 * m + 16 * al
                    to = (slice(16 * code, 16 * (code + 1)), slice(256 * al, 256 * (al + 1)))
                    high_ref[to] = high[at : at + 16, :]
                    low_ref[to] = low[at : at + 16, :]


def message_kernel(keys_ref, guests_ref, high_ref, message_ref, chunk_ref):
    spots = []
    for slot in range(CAP):
        key = keys_ref[:, slot : slot + 1]
        spot = (12 - ((key >> 8) & 15)) * 16 + ((key >> 4) & 15)
        spots.append(jnp.where(key < 0, -1, spot))
    for slot in range(CAP):
        key = guests_ref[:, slot : slot + 1]
        spot = (14 + ((key >> 8) & 15)) * 16 + (key & 15)
        spots.append(jnp.where(key < 0, -1, spot))
    lane = iota((32, 432), 1)
    picks = jnp.concatenate(
        [jnp.where(lane == spot, 1.0, 0.0).astype(jnp.bfloat16) for spot in spots], axis=0
    )
    picked = jnp.dot(picks, high_ref[...], preferred_element_type=jnp.float32)
    for slot in range(2 * CAP):
        for part in range(4):
            chunk_ref[:, 4 * part + slot, :] = picked[
                32 * slot : 32 * (slot + 1), 128 * part : 128 * (part + 1)
            ]
    message_ref[...] = chunk_ref[...].astype(jnp.bfloat16)


def local_kernel(keys_ref, guests_ref, neighbors_ref, high_ref, low_ref, local_ref, place_ref):
    myself = lax.axis_index("box").astype(jnp.int32)
    named = neighbors_ref[...]
    within = named - 16 * myself
    within = jnp.where((within >= 0) & (within < 16), within, -1).astype(jnp.float32)
    within = within.astype(jnp.bfloat16)
    lane = iota((13, 208), 1)
    row = iota((13, 208), 0)
    ahead = jnp.where((lane >> 4) == row, 1.0, 0.0).astype(jnp.bfloat16)
    behind = jnp.where((lane >> 4) == 12 - row, 1.0, 0.0).astype(jnp.bfloat16)
    pull = jnp.dot(within, ahead, preferred_element_type=jnp.float32).astype(jnp.int32)
    push = jnp.dot(within, behind, preferred_element_type=jnp.float32)
    lane = iota((16, 208), 1) & 15
    row = iota((16, 208), 0)
    push = jnp.sum(jnp.where(lane == row, push, 0.0), axis=0, keepdims=True).astype(jnp.int32)
    pull_mask = jnp.where(pull == lane, 1.0, 0.0)
    push_mask = jnp.where(jnp.broadcast_to(push, row.shape) == row, 1.0, 0.0)
    same_mask = jnp.where(iota((16, 16), 0) == iota((16, 16), 1), 1.0, 0.0)
    mask = jnp.concatenate([push_mask, same_mask, pull_mask], axis=1).astype(jnp.bfloat16)
    local = jnp.dot(mask, high_ref[...], preferred_element_type=jnp.float32) + jnp.dot(
        mask, low_ref[...], preferred_element_type=jnp.float32
    )
    for part in range(4):
        local_ref[16 * part : 16 * (part + 1), :] = local[:, 128 * part : 128 * (part + 1)]
    lane = iota((32, 128), 1)
    guests = guests_ref[...]
    keys = jnp.where((lane == 2) | (lane == 3), jnp.roll(keys_ref[...], 2, axis=1), -1)
    target = jnp.where(lane < 2, guests & 15, (keys >> 4) & 15)
    target = jnp.where(jnp.where(lane < 2, guests, keys) < 0, -1, target)
    spread = jnp.where((iota((32, 512), 1) >> 4) == iota((32, 512), 0), 1.0, 0.0)
    target = lax.dot_general(
        target.astype(jnp.float32).astype(jnp.bfloat16),
        spread.astype(jnp.bfloat16),
        (((0,), (0,)), ((), ())),
        preferred_element_type=jnp.float32,
    )[:8]
    lane = iota((8, 512), 1)
    target = jnp.sum(
        jnp.where((lane & 3) == iota((8, 512), 0), target, 0.0), axis=0, keepdims=True
    ).astype(jnp.int32)
    lane = iota((64, 512), 1)
    row = iota((64, 512), 0)
    place = (jnp.broadcast_to(target, lane.shape) == (row & 15)) & (((lane >> 2) & 3) == (row >> 4))
    place_ref[...] = jnp.where(place, 1.0, 0.0).astype(jnp.bfloat16)


def gather_kernel(local_ref, place_ref, arrived_ref, out_ref):
    total = local_ref[...] + jnp.dot(
        place_ref[...], arrived_ref[...].reshape(512, 128), preferred_element_type=jnp.float32
    )
    for part in range(4):
        out_ref[part // 2, :, 128 * (part % 2) : 128 * (part % 2 + 1)] = total[
            16 * part : 16 * (part + 1), :
        ]


def call(kernel, outs, scratch, name, *args):
    vmem = pl.BlockSpec(memory_space=pltpu.VMEM)
    return pl.pallas_call(
        kernel,
        out_shape=outs,
        in_specs=[vmem] * len(args),
        out_specs=jax.tree.map(lambda _: vmem, outs),
        scratch_shapes=scratch,
        name=name,
    )(*args)


def near(value):
    return pltpu.with_memory_space_constraint(value, pltpu.VMEM)


def on_device(coeffs, operators, neighbors):
    degree, box_count, plane_size = coeffs.shape
    groups = lax.axis_size("box")
    terms = lax.axis_size("term")
    shape = pltpu.VMEM
    packed = call(
        pack_kernel,
        shape((terms, degree, 128), jnp.bfloat16),
        [],
        "pack",
        operators.reshape(-1, degree),
    )
    packed = lax.all_to_all(packed, "term", split_axis=0, concat_axis=0, tiled=True)
    keys = call(request_kernel, shape((groups, 128), jnp.int32), [], "request", neighbors)
    guests = lax.all_to_all(keys, "box", split_axis=0, concat_axis=0, tiled=True)
    wide = 2 * plane_size
    image = shape((27 * box_count, wide), jnp.bfloat16)
    high, low = call(
        image_kernel,
        (image, image),
        [
            pltpu.VMEM((128, 1536), jnp.float32),
            pltpu.VMEM((128, 1536), jnp.float32),
            pltpu.VMEM((1536, 256), jnp.bfloat16),
            pltpu.VMEM((96, 4096), jnp.bfloat16),
            pltpu.VMEM((2, 256, 4096), jnp.bfloat16),
        ],
        "image",
        near(packed),
        coeffs.reshape(degree * box_count, plane_size),
    )
    message = call(
        message_kernel,
        shape((groups, 16, 128), jnp.bfloat16),
        [pltpu.VMEM((groups, 16, 128), jnp.float32)],
        "message",
        near(keys),
        near(guests),
        near(high),
    )
    arrived = lax.all_to_all(message, "box", split_axis=0, concat_axis=0, tiled=True)
    local, place = call(
        local_kernel,
        (shape((64, 128), jnp.float32), shape((64, 16 * groups), jnp.bfloat16)),
        [],
        "local",
        near(keys),
        near(guests),
        neighbors,
        near(high),
        near(low),
    )
    return call(
        gather_kernel,
        jax.ShapeDtypeStruct((2, box_count, plane_size), jnp.float32),
        [],
        "gather",
        near(local),
        near(place),
        near(arrived),
    )


def solution(mesh):
    placed = (P(None, "box", None), P("term", None, None, None), P("box", None))
    return jax.shard_map(
        on_device, mesh=mesh, in_specs=placed, out_specs=P("term", "box", None), check_vma=False
    )
```

profile of v0, /device:TPU:1, one launch (start us, length us, event | category | flops | bytes accessed | tf_op | source)
XLA Modules:
  0.0 51.8 jit_solution(2804237256713329505)
XLA Ops:
  0.0 1.4 %pack.1 = bf16[8,16,128]{2,1,0:T(8,128)(2,1)} custom-call(bf16[96,16]{1,0:T(8,128)(2,1)} %bitcast.9), custom_call_target="tpu_custom_call" | custom-call | tf_op jit(solution)/shard_map/pack/pallas_call | solution.py:188
  1.4 9.0 %all-to-all-start.1 = ((bf16[8,16,128]{2,1,0:T(8,128)(2,1)}), bf16[8,16,128]{2,1,0:T(8,128)(2,1)S(1)}, u32[]{:S(2)}, u32[]{:S(2)}) async-start(bf16[8,16,128]{2,1,0:T(8,128)(2,1)} %pack.1), calls=%async_computation.1 | async-start | bytes 65536 | tf_op jit(solution)/shard_map/all_to_all | solution.py:214
  10.4 1.6 %request.1.keys_ref = s32[32,128]{1,0:T(8,128)} custom-call(s32[16,13]{1,0:T(8,128)} %neighbors_ref.3), custom_call_target="tpu_custom_call" | custom-call | tf_op jit(solution)/shard_map/request/pallas_call | solution.py:188
  12.0 5.3 %all-to-all-done.1.packed_ref = bf16[8,16,128]{2,1,0:T(8,128)(2,1)S(1)} async-done(((bf16[8,16,128]{2,1,0:T(8,128)(2,1)}), bf16[8,16,128]{2,1,0:T(8,128)(2,1)S(1)}, u32[]{:S(2)}, u32[]{:S(2)}) %all-to-all-start.1) | async-done | bytes 32800 | tf_op jit(solution)/shard_map/all_to_all | solution.py:214
  17.3 9.2 %all-to-all-start = ((s32[32,1,128]{2,1,0:T(1,128)}), s32[32,1,128]{2,1,0:T(1,128)S(1)}, u32[]{:S(2)}, u32[]{:S(2)}) async-start(s32[32,1,128]{2,1,0:T(1,128)} %bitcast.1), calls=%async_computation | async-start | bytes 32768 | tf_op jit(solution)/shard_map/all_to_all | solution.py:216
  26.5 7.7 %image.1 = (bf16[432,512]{1,0:T(8,128)(2,1)S(1)}, bf16[432,512]{1,0:T(8,128)(2,1)S(1)}) custom-call(bf16[8,16,128]{2,1,0:T(8,128)(2,1)S(1)} %all-to-all-done.1.packed_ref, bf16[256,256]{1,0:T(8,128)(2,1)} %bitcast.8), custom_call_target="tpu_custom_call" | custom-call | tf_op jit(solution)/shard_map/image/pallas_call | solution.py:188
  34.2 0.0 all-to-all-done
  34.2 1.8 %message.1 = bf16[32,16,128]{2,1,0:T(8,128)(2,1)} custom-call(s32[32,128]{1,0:T(8,128)} %request.1.keys_ref, s32[32,128]{1,0:T(8,128)S(1)} %bitcast.6, bf16[432,512]{1,0:T(8,128)(2,1)S(1)} %get-tuple-element.9.high_ref), custom_call_target="tpu_custom_call" | custom-call | tf_op jit(solution)/shard_map/message/pallas_call | solution.py:188
  36.0 7.4 %all-to-all-start.2 = ((bf16[32,16,128]{2,1,0:T(8,128)(2,1)}), bf16[32,16,128]{2,1,0:T(8,128)(2,1)S(1)}, u32[]{:S(2)}, u32[]{:S(2)}) async-start(bf16[32,16,128]{2,1,0:T(8,128)(2,1)} %message.1), calls=%async_computation.2 | async-start | bytes 262144 | tf_op jit(solution)/shard_map/all_to_all | solution.py:242
  43.4 1.2 %local.1 = (f32[64,128]{1,0:T(8,128)S(1)}, bf16[64,512]{1,0:T(8,128)(2,1)S(1)}) custom-call(s32[32,128]{1,0:T(8,128)} %request.1.keys_ref, s32[32,128]{1,0:T(8,128)S(1)} %bitcast.7, s32[16,13]{1,0:T(8,128)} %neighbors_ref.3, bf16[432,512]{1,0:T(8,128)(2,1)S(1)} %get-tuple-element.9.high_ref, bf16[432,512]{1,0:T(8,128)(2,1)S(1)} %get-tuple-element.10.low_ref), custom_call_target="tpu_custom_call" | custom-call | tf_op jit(solution)/shard_map/local/pallas_call | solution.py:188
  44.6 6.4 %all-to-all-done.2.arrived_ref = bf16[32,16,128]{2,1,0:T(8,128)(2,1)S(1)} async-done(((bf16[32,16,128]{2,1,0:T(8,128)(2,1)}), bf16[32,16,128]{2,1,0:T(8,128)(2,1)S(1)}, u32[]{:S(2)}, u32[]{:S(2)}) %all-to-all-start.2) | async-done | bytes 131104 | tf_op jit(solution)/shard_map/all_to_all | solution.py:242
  51.0 0.8 %gather.1 = f32[2,16,256]{2,1,0:T(8,128)} custom-call(f32[64,128]{1,0:T(8,128)S(1)} %get-tuple-element.11.local_ref, bf16[64,512]{1,0:T(8,128)(2,1)S(1)} %get-tuple-element.12.place_ref, bf16[32,16,128]{2,1,0:T(8,128)(2,1)S(1)} %all-to-all-done.2.arrived_ref), custom_call_target="tpu_custom_call" | custom-call | tf_op jit(solution)/shard_map/gather/pallas_call | solution.py:188
Async XLA Ops:
  1.4 15.9 %all-to-all-start.1 = ((bf16[8,16,128]{2,1,0:T(8,128)(2,1)}), bf16[8,16,128]{2,1,0:T(8,128)(2,1)S(1)}, u32[]{:S(2)}, u32[]{:S(2)}) async-start(bf16[8,16,128]{2,1,0:T(8,128)(2,1)} %pack.1), calls=%async_computation.1 | async-start | bytes 65536 | tf_op jit(solution)/shard_map/all_to_all | solution.py:214
  17.3 16.9 %all-to-all-start = ((s32[32,1,128]{2,1,0:T(1,128)}), s32[32,1,128]{2,1,0:T(1,128)S(1)}, u32[]{:S(2)}, u32[]{:S(2)}) async-start(s32[32,1,128]{2,1,0:T(1,128)} %bitcast.1), calls=%async_computation | async-start | bytes 32768 | tf_op jit(solution)/shard_map/all_to_all | solution.py:216
  36.0 15.0 %all-to-all-start.2 = ((bf16[32,16,128]{2,1,0:T(8,128)(2,1)}), bf16[32,16,128]{2,1,0:T(8,128)(2,1)S(1)}, u32[]{:S(2)}, u32[]{:S(2)}) async-start(bf16[32,16,128]{2,1,0:T(8,128)(2,1)} %message.1), calls=%async_computation.2 | async-start | bytes 262144 | tf_op jit(solution)/shard_map/all_to_all | solution.py:242
where the time goes:
time: 52.3 us; the launch traced here: 51.8 us
  starting transfers between devices  25.6 us (49%)
  Pallas kernels  14.4 us (28%)
  waiting for transfers between devices  11.7 us (22%)
    pallas_call x6, Pallas kernels, call(): pl.pallas_call(kernel, out_shape=outs, in_specs=[vmem] * len(args), out_s...  14.4 us
    all_to_all x1, starting transfers between devices, on_device(): lax.all_to_all(keys, 'box', split_axis=0, concat_axis=0, tiled=True)  9.19 us
    all_to_all x1, starting transfers between devices, on_device(): lax.all_to_all(packed, 'term', split_axis=0, concat_axis=0, tiled=True)  9 us
    all_to_all x1, starting transfers between devices, on_device(): lax.all_to_all(message, 'box', split_axis=0, concat_axis=0, tiled=True)  7.38 us
    all_to_all x1, waiting for transfers between devices, on_device(): lax.all_to_all(message, 'box', split_axis=0, concat_axis=0, tiled=True)  6.43 us
    all_to_all x1, waiting for transfers between devices, on_device(): lax.all_to_all(packed, 'term', split_axis=0, concat_axis=0, tiled=True)  5.31 us
  transfers between devices with their start and end apart: 3, of which 2 were waited for; matrix products, arithmetic and copies ran while one was open for 0% of the time, Pallas kernels for 20%

commit v1 on v0

--- a/solution.py
+++ b/solution.py
@@ -1,3 +1,5 @@
+import functools
+
 import jax
 import jax.numpy as jnp
 from jax import lax
@@ -6,6 +8,7 @@
 from jax.sharding import PartitionSpec as P
 
 CAP = 2
+GROUP = 4
 BIG = 0x7FFFFFFF
 
 
@@ -13,7 +16,8 @@
     return lax.broadcasted_iota(jnp.int32, shape, axis)
 
 
-def request_kernel(neighbors_ref, keys_ref):
+def request_kernel(neighbors_ref, operators_ref, keys_ref, mine_ref):
+    mine_ref[...] = operators_ref[...]
     box_count, column_count = neighbors_ref.shape
     groups = keys_ref.shape[0]
     myself = lax.axis_index("box").astype(jnp.int32)
@@ -37,71 +41,74 @@
     keys_ref[...] = jnp.where(lane == 0, first, jnp.where(lane == 1, last, -1))
 
 
-def pack_kernel(operators_ref, packed_ref):
-    blocks = [operators_ref[16 * i : 16 * (i + 1), :] for i in range(6)]
-    pad = jnp.zeros((16, 32), operators_ref.dtype)
-    row = jnp.concatenate(blocks + [pad], axis=1)
-    for i in range(packed_ref.shape[0]):
-        packed_ref[i] = row
-
-
-def expand(rows, modulo):
-    lane = iota((128, 1536), 1)
-    row = iota((128, 1536), 0)
-    pick = ((lane >> 8) << 4) + ((lane & 15) if modulo else ((lane >> 4) & 15))
-    ones = jnp.where(pick == row, 1.0, 0.0).astype(jnp.bfloat16)
-    return jnp.dot(rows, ones, preferred_element_type=jnp.float32)
-
-
-def image_kernel(
-    packed_ref, coeffs_ref, high_ref, low_ref, outer_ref, inner_ref, left_ref, half_ref, kron_ref
-):
+def image_kernel(terms, pieces, first, final, coeffs_ref, *refs):
+    rows_refs, refs = refs[:pieces], list(refs[pieces:])
+    before_ref = None if first else refs.pop(0)
+    after_ref = None if final else refs.pop(0)
+    high_ref, low_ref = (refs.pop(0), refs.pop(0)) if final else (None, None)
+    outer_ref, inner_ref, left_ref, half_ref, kron_ref = refs[:5]
+    sum_ref = refs[5] if final else after_ref
     term = lax.axis_index("term").astype(jnp.int32)
-    rows = packed_ref[...].reshape(128, 128)
-    outer_ref[...] = expand(rows, False)
-    inner_ref[...] = expand(rows, True)
-    diagonal = (iota((16, 256), 1) & 15) == iota((16, 256), 0)
-    for r in range(16):
-        d, e = divmod(r, 2)
+    lane = iota((16, 256), 1)
+    row = iota((16, 256), 0)
+    to_outer = jnp.where((lane >> 4) == row, 1.0, 0.0).astype(jnp.bfloat16)
+    to_inner = jnp.where((lane & 15) == row, 1.0, 0.0).astype(jnp.bfloat16)
+    rows = jnp.concatenate([ref[...] for ref in rows_refs], axis=0)
+    outer_ref[...] = jnp.dot(rows, to_outer, preferred_element_type=jnp.float32)
+    inner_ref[...] = jnp.dot(rows, to_inner, preferred_element_type=jnp.float32).astype(
+        jnp.bfloat16
+    )
+    diagonal = (lane & 15) == row
+    for r in range(terms):
         for m in range(3):
-            lanes = slice(256 * (3 * e + m), 256 * (3 * e + m + 1))
             for al in range(2):
-                row = outer_ref[pl.ds(16 * d + 2 * term + al, 1), lanes]
-                block = jnp.where(diagonal, jnp.broadcast_to(row, (16, 256)), 0.0)
+                line = outer_ref[pl.ds(16 * (3 * r + m) + 2 * term + al, 1), :]
+                block = jnp.where(diagonal, jnp.broadcast_to(line, (16, 256)), 0.0)
                 at = 96 * r + 32 * m + 16 * al
                 left_ref[at : at + 16, :] = block.astype(jnp.bfloat16)
     half = jnp.dot(left_ref[...], coeffs_ref[...], preferred_element_type=jnp.float32)
     half = half.astype(jnp.bfloat16)
-    for r in range(16):
+    for r in range(terms):
         half_ref[:, 256 * r : 256 * (r + 1)] = half[96 * r : 96 * (r + 1), :]
-    for n in range(3):
-        for p in range(3):
-            slot = (3 * n + p) % 2
-            for r in range(16):
-                d, e = divmod(r, 2)
-                at = 3 * e + n
-                outer = outer_ref[16 * d : 16 * (d + 1), 256 * at : 256 * (at + 1)]
-                at = 3 * e + p
-                inner = inner_ref[16 * d : 16 * (d + 1), 256 * at : 256 * (at + 1)]
-                product = outer[:, None, :] * inner[None, :, :]
-                kron_ref[slot, :, 256 * r : 256 * (r + 1)] = product.reshape(256, 256).astype(
-                    jnp.bfloat16
+    wide = 256 * GROUP
+    for start in range(0, terms, GROUP):
+        last = start + GROUP == terms
+        for n in range(3):
+            slot = 3 * ((3 * (start // GROUP) + n) % 2)
+            for r in range(start, start + GROUP):
+                to = slice(256 * (r - start), 256 * (r - start + 1))
+                inner = [
+                    inner_ref[16 * (3 * r + p) : 16 * (3 * r + p + 1), :] for p in range(3)
+                ]
+                for a in range(16):
+                    at = 16 * (3 * r + n) + a
+                    line = outer_ref[at : at + 1, :]
+                    line = jnp.broadcast_to(line, (16, 256)).astype(jnp.bfloat16)
+                    for p in range(3):
+                        kron_ref[slot + p, 16 * a : 16 * (a + 1), to] = line * inner[p]
+            for p in range(3):
+                applied = lax.dot_general(
+                    half_ref[:, 256 * start : 256 * start + wide],
+                    kron_ref[slot + p],
+                    (((1,), (1,)), ((), ())),
+                    preferred_element_type=jnp.float32,
                 )
-            applied = lax.dot_general(
-                half_ref[...],
-                kron_ref[slot],
-                (((1,), (1,)), ((), ())),
-                preferred_element_type=jnp.float32,
-            )
-            high = applied.astype(jnp.bfloat16)
-            low = (applied - high.astype(jnp.float32)).astype(jnp.bfloat16)
-            for m in range(3):
-                code = 9 * m + 3 * n + p
-                for al in range(2):
-                    at = 32 * m + 16 * al
-                    to = (slice(16 * code, 16 * (code + 1)), slice(256 * al, 256 * (al + 1)))
-                    high_ref[to] = high[at : at + 16, :]
-                    low_ref[to] = low[at : at + 16, :]
+                if start:
+                    applied = applied + sum_ref[3 * n + p]
+                elif not first:
+                    applied = applied + before_ref[3 * n + p]
+                if not (final and last):
+                    sum_ref[3 * n + p] = applied
+                    continue
+                high = applied.astype(jnp.bfloat16)
+                low = (applied - high.astype(jnp.float32)).astype(jnp.bfloat16)
+                for m in range(3):
+                    code = 9 * m + 3 * n + p
+                    for al in range(2):
+                        at = 32 * m + 16 * al
+                        to = (slice(16 * code, 16 * (code + 1)), slice(256 * al, 256 * (al + 1)))
+                        high_ref[to] = high[at : at + 16, :]
+                        low_ref[to] = low[at : at + 16, :]
 
 
 def message_kernel(keys_ref, guests_ref, high_ref, message_ref, chunk_ref):
@@ -183,7 +190,7 @@
         ]
 
 
-def call(kernel, outs, scratch, name, *args):
+def call(kernel, outs, scratch, *args):
     vmem = pl.BlockSpec(memory_space=pltpu.VMEM)
     return pl.pallas_call(
         kernel,
@@ -191,7 +198,6 @@
         in_specs=[vmem] * len(args),
         out_specs=jax.tree.map(lambda _: vmem, outs),
         scratch_shapes=scratch,
-        name=name,
     )(*args)
 
 
@@ -204,37 +210,55 @@
     groups = lax.axis_size("box")
     terms = lax.axis_size("term")
     shape = pltpu.VMEM
-    packed = call(
-        pack_kernel,
-        shape((terms, degree, 128), jnp.bfloat16),
+    coeffs = near(coeffs.reshape(degree * box_count, plane_size))
+    totals = shape((9, 6 * box_count, plane_size), jnp.float32)
+    image = shape((27 * box_count, 2 * plane_size), jnp.bfloat16)
+
+    def swap(value, bit):
+        return lax.ppermute(value, "term", [(i, i ^ bit) for i in range(terms)])
+
+    def images(rows, before, final):
+        height = sum(piece.shape[0] for piece in rows)
+        count = height // (3 * degree)
+        scratch = [
+            pltpu.VMEM((height, plane_size), jnp.float32),
+            pltpu.VMEM((height, plane_size), jnp.bfloat16),
+            pltpu.VMEM((6 * box_count * count, plane_size), jnp.bfloat16),
+            pltpu.VMEM((6 * box_count, plane_size * count), jnp.bfloat16),
+            pltpu.VMEM((6, plane_size, plane_size * GROUP), jnp.bfloat16),
+        ]
+        if final:
+            scratch.append(pltpu.VMEM((9, 6 * box_count, plane_size), jnp.float32))
+        return call(
+            functools.partial(image_kernel, count, len(rows), before is None, final),
+            (image, image) if final else totals,
+            scratch,
+            coeffs,
+            *[near(piece) for piece in rows],
+            *([] if before is None else [near(before)]),
+        )
+
+    mine = operators.reshape(-1, degree)
+    other = swap(mine, 4)
+    keys, pair = call(
+        request_kernel,
+        (shape((groups, 128), jnp.int32), shape(mine.shape, mine.dtype)),
         [],
-        "pack",
-        operators.reshape(-1, degree),
-    )
-    packed = lax.all_to_all(packed, "term", split_axis=0, concat_axis=0, tiled=True)
-    keys = call(request_kernel, shape((groups, 128), jnp.int32), [], "request", neighbors)
+        neighbors,
+        mine,
+    )
     guests = lax.all_to_all(keys, "box", split_axis=0, concat_axis=0, tiled=True)
-    wide = 2 * plane_size
-    image = shape((27 * box_count, wide), jnp.bfloat16)
-    high, low = call(
-        image_kernel,
-        (image, image),
-        [
-            pltpu.VMEM((128, 1536), jnp.float32),
-            pltpu.VMEM((128, 1536), jnp.float32),
-            pltpu.VMEM((1536, 256), jnp.bfloat16),
-            pltpu.VMEM((96, 4096), jnp.bfloat16),
-            pltpu.VMEM((2, 256, 4096), jnp.bfloat16),
-        ],
-        "image",
-        near(packed),
-        coeffs.reshape(degree * box_count, plane_size),
-    )
+    pair = jnp.concatenate([pair, other], axis=0)
+    ones = swap(pair, 1)
+    twos = swap(pair, 2)
+    threes = swap(pair, 3)
+    total = images([pair], None, False)
+    total = images([ones], total, False)
+    high, low = images([twos, threes], total, True)
     message = call(
         message_kernel,
         shape((groups, 16, 128), jnp.bfloat16),
         [pltpu.VMEM((groups, 16, 128), jnp.float32)],
-        "message",
         near(keys),
         near(guests),
         near(high),
@@ -244,7 +268,6 @@
         local_kernel,
         (shape((64, 128), jnp.float32), shape((64, 16 * groups), jnp.bfloat16)),
         [],
-        "local",
         near(keys),
         near(guests),
         neighbors,
@@ -255,7 +278,6 @@
         gather_kernel,
         jax.ShapeDtypeStruct((2, box_count, plane_size), jnp.float32),
         [],
-        "gather",
         near(local),
         near(place),
         near(arrived),

time: 52.3 us -> 47.1 us (0.901)
  waiting for transfers between devices: 11.7 us -> 6.45 us
  starting transfers between devices: 25.6 us -> 28.2 us
  Pallas kernels: 14.4 us -> 11.9 us
    ppermute x0 -> x4, starting transfers between devices: none -> 11.4 us  [swap(): return lax.ppermute(value, 'term', [(i, i ^ bit) for i in range(terms)])]
    all_to_all x1 -> x0, starting transfers between devices: 9 us -> none  [on_device(): lax.all_to_all(packed, 'term', split_axis=0, concat_axis=0, tiled=True)]
    all_to_all x1 -> x0, waiting for transfers between devices: 5.31 us -> none  [on_device(): lax.all_to_all(packed, 'term', split_axis=0, concat_axis=0, tiled=True)]
    pallas_call x6 -> x7, Pallas kernels: 14.4 us -> 11.9 us  [call(): pl.pallas_call(kernel, out_shape=outs, in_specs=[vmem] * len(args), out_s...]
    all_to_all x1, starting transfers between devices: 7.38 us -> 8.82 us  [on_device(): lax.all_to_all(message, 'box', split_axis=0, concat_axis=0, tiled=True)]
    all_to_all x1, starting transfers between devices: 9.19 us -> 8.04 us  [on_device(): lax.all_to_all(keys, 'box', split_axis=0, concat_axis=0, tiled=True)]
  transfers between devices with their start and end apart: 3 -> 6, of which waited for: 2 -> 1; matrix products, arithmetic and copies ran while one was open for 0% -> 0% of each run, Pallas kernels for 20% -> 20%
where the time goes in v1:
time: 47.1 us; the launch traced here: 46.6 us
  starting transfers between devices  28.2 us (60%)
  Pallas kernels  11.9 us (25%)
  waiting for transfers between devices  6.45 us (14%)
    pallas_call x7, Pallas kernels, call(): pl.pallas_call(kernel, out_shape=outs, in_specs=[vmem] * len(args), out_s...  11.9 us
    ppermute x4, starting transfers between devices, swap(): return lax.ppermute(value, 'term', [(i, i ^ bit) for i in range(terms)])  11.4 us
    all_to_all x1, starting transfers between devices, on_device(): lax.all_to_all(message, 'box', split_axis=0, concat_axis=0, tiled=True)  8.82 us
    all_to_all x1, starting transfers between devices, on_device(): lax.all_to_all(keys, 'box', split_axis=0, concat_axis=0, tiled=True)  8.04 us
    all_to_all x1, waiting for transfers between devices, on_device(): lax.all_to_all(message, 'box', split_axis=0, concat_axis=0, tiled=True)  6.43 us
  transfers between devices with their start and end apart: 6, of which 1 were waited for; matrix products, arithmetic and copies ran while one was open for 0% of the time, Pallas kernels for 20%

profile of v1, /device:TPU:1, one launch (start us, length us, event | category | flops | bytes accessed | tf_op | source)
XLA Modules:
  0.0 46.6 jit_solution(16176617400260035515)
XLA Ops:
  0.0 0.0 copy-start
  0.0 7.7 %collective-permute-start = (bf16[96,16]{1,0:T(8,128)(2,1)}, bf16[96,16]{1,0:T(8,128)(2,1)S(1)}, u32[]{:S(2)}, u32[]{:S(2)}) collective-permute-start(bf16[96,16]{1,0:T(8,128)(2,1)} %bitcast.11), channel_id=1, source_target_pairs={{0,4},{1,5},{2,6},{3,7},{4,0},{5,1},{6,2},{7,3},{8,12},{9,13},{10,... | collective-permute-start | bytes 9224 | tf_op jit(solution)/shard_map/ppermute | solution.py:218
  7.7 1.7 %shard_map.37 = (s32[32,128]{1,0:T(8,128)}, bf16[96,16]{1,0:T(8,128)(2,1)S(1)}) custom-call(s32[16,13]{1,0:T(8,128)} %neighbors_ref.3, bf16[96,16]{1,0:T(8,128)(2,1)} %bitcast.12), custom_call_target="tpu_custom_call" | custom-call | tf_op jit(solution)/shard_map/pallas_call | solution.py:195
  9.4 8.0 %all-to-all-start = ((s32[32,1,128]{2,1,0:T(1,128)}), s32[32,1,128]{2,1,0:T(1,128)S(1)}, u32[]{:S(2)}, u32[]{:S(2)}) async-start(s32[32,1,128]{2,1,0:T(1,128)} %bitcast.2), calls=%async_computation | async-start | bytes 32768 | tf_op jit(solution)/shard_map/all_to_all | solution.py:250
  17.4 0.0 collective-permute-done
  17.5 0.8 %collective-permute-start.3 = (bf16[192,16]{1,0:T(8,128)(2,1)S(1)}, bf16[192,16]{1,0:T(8,128)(2,1)S(1)}, u32[]{:S(2)}, u32[]{:S(2)}) collective-permute-start(bf16[192,16]{1,0:T(8,128)(2,1)S(1)} %constant_dynamic-update-slice_fusion.refs_0_), channel_id=1, source_target_pairs={{0,1},{1,0},{2,3},{3,2},{4,5},{5,4},{6,7},{7,6},{8,9},{9,8},{10,11... | collective-permute-start | bytes 18440 | tf_op jit(solution)/shard_map/ppermute | solution.py:218
  18.3 1.2 %collective-permute-start.1 = (bf16[192,16]{1,0:T(8,128)(2,1)S(1)}, bf16[192,16]{1,0:T(8,128)(2,1)S(1)}, u32[]{:S(2)}, u32[]{:S(2)}) collective-permute-start(bf16[192,16]{1,0:T(8,128)(2,1)S(1)} %constant_dynamic-update-slice_fusion.refs_0_), channel_id=1, source_target_pairs={{0,2},{1,3},{2,0},{3,1},{4,6},{5,7},{6,4},{7,5},{8,10},{9,11},{10,... | collective-permute-start | bytes 18440 | tf_op jit(solution)/shard_map/ppermute | solution.py:218
  19.5 1.6 %collective-permute-start.2 = (bf16[192,16]{1,0:T(8,128)(2,1)S(1)}, bf16[192,16]{1,0:T(8,128)(2,1)S(1)}, u32[]{:S(2)}, u32[]{:S(2)}) collective-permute-start(bf16[192,16]{1,0:T(8,128)(2,1)S(1)} %constant_dynamic-update-slice_fusion.refs_0_), channel_id=1, source_target_pairs={{0,3},{1,2},{2,1},{3,0},{4,7},{5,6},{6,5},{7,4},{8,11},{9,10},{10,... | collective-permute-start | bytes 18440 | tf_op jit(solution)/shard_map/ppermute | solution.py:218
  21.1 0.0 copy-done
  21.1 1.7 %shard_map.38.refs_1_ = f32[9,96,256]{2,1,0:T(8,128)S(1)} custom-call(bf16[256,256]{1,0:T(8,128)(2,1)S(1)} %bitcast.6, bf16[192,16]{1,0:T(8,128)(2,1)S(1)} %constant_dynamic-update-slice_fusion.refs_0_), custom_call_target="tpu_custom_call" | custom-call | tf_op jit(solution)/shard_map/pallas_call | solution.py:195
  22.8 0.0 collective-permute-done.3.refs_0_
  22.8 1.7 %shard_map.39.refs_2_ = f32[9,96,256]{2,1,0:T(8,128)S(1)} custom-call(bf16[256,256]{1,0:T(8,128)(2,1)S(1)} %bitcast.7, bf16[192,16]{1,0:T(8,128)(2,1)S(1)} %collective-permute-done.3.refs_0_, f32[9,96,256]{2,1,0:T(8,128)S(1)} %shard_map.38.refs_1_), custom_call_target="tpu_custom_call" | custom-call | tf_op jit(solution)/shard_map/pallas_call | solution.py:195
  24.6 0.0 collective-permute-done.1.refs_0_
  24.6 0.0 collective-permute-done.2.refs_1_
  24.6 3.1 %shard_map.40 = (bf16[432,512]{1,0:T(8,128)(2,1)S(1)}, bf16[432,512]{1,0:T(8,128)(2,1)S(1)}) custom-call(bf16[256,256]{1,0:T(8,128)(2,1)S(1)} %bitcast.8, bf16[192,16]{1,0:T(8,128)(2,1)S(1)} %collective-permute-done.1.refs_0_, bf16[192,16]{1,0:T(8,128)(2,1)S(1)} %collective-permute-done.2.refs_1_, f32[9,96,256]{2,1,0:T(8,128)S(1)} %shard_map.39.refs_2_), custom_call_target="tpu_custom_call" | custom-call | tf_op jit(solution)/shard_map/pallas_call | solution.py:195
  27.7 0.0 all-to-all-done
  27.7 1.8 %shard_map.42 = bf16[32,16,128]{2,1,0:T(8,128)(2,1)} custom-call(s32[32,128]{1,0:T(8,128)} %get-tuple-element.11.keys_ref, s32[32,128]{1,0:T(8,128)S(1)} %bitcast.9, bf16[432,512]{1,0:T(8,128)(2,1)S(1)} %get-tuple-element.13.high_ref), custom_call_target="tpu_custom_call" | custom-call | tf_op jit(solution)/shard_map/pallas_call | solution.py:195
  29.4 8.8 %all-to-all-start.1 = ((bf16[32,16,128]{2,1,0:T(8,128)(2,1)}), bf16[32,16,128]{2,1,0:T(8,128)(2,1)S(1)}, u32[]{:S(2)}, u32[]{:S(2)}) async-start(bf16[32,16,128]{2,1,0:T(8,128)(2,1)} %shard_map.42), calls=%async_computation.1 | async-start | bytes 262144 | tf_op jit(solution)/shard_map/all_to_all | solution.py:266
  38.3 1.2 %shard_map.41 = (f32[64,128]{1,0:T(8,128)S(1)}, bf16[64,512]{1,0:T(8,128)(2,1)S(1)}) custom-call(s32[32,128]{1,0:T(8,128)} %get-tuple-element.11.keys_ref, s32[32,128]{1,0:T(8,128)S(1)} %bitcast.10, s32[16,13]{1,0:T(8,128)} %neighbors_ref.3, bf16[432,512]{1,0:T(8,128)(2,1)S(1)} %get-tuple-element.13.high_ref, bf16[432,512]{1,0:T(8,128)(2,1)S(1)} %get-tuple-element.14.low_ref), custom_call_target="tpu_custom_call" | custom-call | tf_op jit(solution)/shard_map/pallas_call | solution.py:195
  39.4 6.4 %all-to-all-done.1.arrived_ref = bf16[32,16,128]{2,1,0:T(8,128)(2,1)S(1)} async-done(((bf16[32,16,128]{2,1,0:T(8,128)(2,1)}), bf16[32,16,128]{2,1,0:T(8,128)(2,1)S(1)}, u32[]{:S(2)}, u32[]{:S(2)}) %all-to-all-start.1) | async-done | bytes 131104 | tf_op jit(solution)/shard_map/all_to_all | solution.py:266
  45.9 0.8 %shard_map.43 = f32[2,16,256]{2,1,0:T(8,128)} custom-call(f32[64,128]{1,0:T(8,128)S(1)} %get-tuple-element.15.local_ref, bf16[64,512]{1,0:T(8,128)(2,1)S(1)} %get-tuple-element.16.place_ref, bf16[32,16,128]{2,1,0:T(8,128)(2,1)S(1)} %all-to-all-done.1.arrived_ref), custom_call_target="tpu_custom_call" | custom-call | tf_op jit(solution)/shard_map/pallas_call | solution.py:195
  (2 shorter events, 0.0 us)
Async XLA Ops:
  0.0 21.1 %copy-start = (bf16[16,16,256]{2,1,0:T(8,128)(2,1)S(1)}, bf16[16,16,256]{2,1,0:T(8,128)(2,1)}, u32[]{:S(2)}) copy-start(bf16[16,16,256]{2,1,0:T(8,128)(2,1)} %param.3) | copy-start | bytes 393220
  0.0 17.4 %collective-permute-start = (bf16[96,16]{1,0:T(8,128)(2,1)}, bf16[96,16]{1,0:T(8,128)(2,1)S(1)}, u32[]{:S(2)}, u32[]{:S(2)}) collective-permute-start(bf16[96,16]{1,0:T(8,128)(2,1)} %bitcast.11), channel_id=1, source_target_pairs={{0,4},{1,5},{2,6},{3,7},{4,0},{5,1},{6,2},{7,3},{8,12},{9,13},{10,... | collective-permute-start | bytes 9224 | tf_op jit(solution)/shard_map/ppermute | solution.py:218
  9.4 18.3 %all-to-all-start = ((s32[32,1,128]{2,1,0:T(1,128)}), s32[32,1,128]{2,1,0:T(1,128)S(1)}, u32[]{:S(2)}, u32[]{:S(2)}) async-start(s32[32,1,128]{2,1,0:T(1,128)} %bitcast.2), calls=%async_computation | async-start | bytes 32768 | tf_op jit(solution)/shard_map/all_to_all | solution.py:250
  17.5 5.4 %collective-permute-start.3 = (bf16[192,16]{1,0:T(8,128)(2,1)S(1)}, bf16[192,16]{1,0:T(8,128)(2,1)S(1)}, u32[]{:S(2)}, u32[]{:S(2)}) collective-permute-start(bf16[192,16]{1,0:T(8,128)(2,1)S(1)} %constant_dynamic-update-slice_fusion.refs_0_), channel_id=1, source_target_pairs={{0,1},{1,0},{2,3},{3,2},{4,5},{5,4},{6,7},{7,6},{8,9},{9,8},{10,11... | collective-permute-start | bytes 18440 | tf_op jit(solution)/shard_map/ppermute | solution.py:218
  18.3 6.3 %collective-permute-start.1 = (bf16[192,16]{1,0:T(8,128)(2,1)S(1)}, bf16[192,16]{1,0:T(8,128)(2,1)S(1)}, u32[]{:S(2)}, u32[]{:S(2)}) collective-permute-start(bf16[192,16]{1,0:T(8,128)(2,1)S(1)} %constant_dynamic-update-slice_fusion.refs_0_), channel_id=1, source_target_pairs={{0,2},{1,3},{2,0},{3,1},{4,6},{5,7},{6,4},{7,5},{8,10},{9,11},{10,... | collective-permute-start | bytes 18440 | tf_op jit(solution)/shard_map/ppermute | solution.py:218
  19.5 5.1 %collective-permute-start.2 = (bf16[192,16]{1,0:T(8,128)(2,1)S(1)}, bf16[192,16]{1,0:T(8,128)(2,1)S(1)}, u32[]{:S(2)}, u32[]{:S(2)}) collective-permute-start(bf16[192,16]{1,0:T(8,128)(2,1)S(1)} %constant_dynamic-update-slice_fusion.refs_0_), channel_id=1, source_target_pairs={{0,3},{1,2},{2,1},{3,0},{4,7},{5,6},{6,5},{7,4},{8,11},{9,10},{10,... | collective-permute-start | bytes 18440 | tf_op jit(solution)/shard_map/ppermute | solution.py:218
  29.4 16.4 %all-to-all-start.1 = ((bf16[32,16,128]{2,1,0:T(8,128)(2,1)}), bf16[32,16,128]{2,1,0:T(8,128)(2,1)S(1)}, u32[]{:S(2)}, u32[]{:S(2)}) async-start(bf16[32,16,128]{2,1,0:T(8,128)(2,1)} %shard_map.42), calls=%async_computation.1 | async-start | bytes 262144 | tf_op jit(solution)/shard_map/all_to_all | solution.py:266

commit v2 on v1

--- a/solution.py
+++ b/solution.py
@@ -111,7 +111,17 @@
                         low_ref[to] = low[at : at + 16, :]
 
 
-def message_kernel(keys_ref, guests_ref, high_ref, message_ref, chunk_ref):
+def message_kernel(
+    keys_ref,
+    guests_ref,
+    neighbors_ref,
+    high_ref,
+    low_ref,
+    message_ref,
+    local_ref,
+    place_ref,
+    chunk_ref,
+):
     spots = []
     for slot in range(CAP):
         key = keys_ref[:, slot : slot + 1]
@@ -132,9 +142,6 @@
                 32 * slot : 32 * (slot + 1), 128 * part : 128 * (part + 1)
             ]
     message_ref[...] = chunk_ref[...].astype(jnp.bfloat16)
-
-
-def local_kernel(keys_ref, guests_ref, neighbors_ref, high_ref, low_ref, local_ref, place_ref):
     myself = lax.axis_index("box").astype(jnp.int32)
     named = neighbors_ref[...]
     within = named - 16 * myself
@@ -214,8 +221,8 @@
     totals = shape((9, 6 * box_count, plane_size), jnp.float32)
     image = shape((27 * box_count, 2 * plane_size), jnp.bfloat16)
 
-    def swap(value, bit):
-        return lax.ppermute(value, "term", [(i, i ^ bit) for i in range(terms)])
+    def swap(value, other):
+        return lax.ppermute(value, "term", [(i, other(i) % terms) for i in range(terms)])
 
     def images(rows, before, final):
         height = sum(piece.shape[0] for piece in rows)
@@ -239,7 +246,7 @@
         )
 
     mine = operators.reshape(-1, degree)
-    other = swap(mine, 4)
+    other = swap(mine, lambda i: i ^ 4)
     keys, pair = call(
         request_kernel,
         (shape((groups, 128), jnp.int32), shape(mine.shape, mine.dtype)),
@@ -249,31 +256,27 @@
     )
     guests = lax.all_to_all(keys, "box", split_axis=0, concat_axis=0, tiled=True)
     pair = jnp.concatenate([pair, other], axis=0)
-    ones = swap(pair, 1)
-    twos = swap(pair, 2)
-    threes = swap(pair, 3)
+    ones = swap(pair, lambda i: i ^ 1)
+    twos = swap(pair, lambda i: i ^ 2)
+    threes = swap(pair, lambda i: i + (1 if i % 2 else -1))
     total = images([pair], None, False)
     total = images([ones], total, False)
     high, low = images([twos, threes], total, True)
-    message = call(
+    message, local, place = call(
         message_kernel,
-        shape((groups, 16, 128), jnp.bfloat16),
+        (
+            shape((groups, 16, 128), jnp.bfloat16),
+            shape((64, 128), jnp.float32),
+            shape((64, 16 * groups), jnp.bfloat16),
+        ),
         [pltpu.VMEM((groups, 16, 128), jnp.float32)],
         near(keys),
         near(guests),
-        near(high),
-    )
-    arrived = lax.all_to_all(message, "box", split_axis=0, concat_axis=0, tiled=True)
-    local, place = call(
-        local_kernel,
-        (shape((64, 128), jnp.float32), shape((64, 16 * groups), jnp.bfloat16)),
-        [],
-        near(keys),
-        near(guests),
-        neighbors,
+        near(neighbors),
         near(high),
         near(low),
     )
+    arrived = lax.all_to_all(message, "box", split_axis=0, concat_axis=0, tiled=True)
     return call(
         gather_kernel,
         jax.ShapeDtypeStruct((2, box_count, plane_size), jnp.float32),

time: 47.1 us -> 45.7 us (0.970)
  blocking collectives: 0 us -> 16.2 us
  starting transfers between devices: 28.2 us -> 17.8 us
  waiting for transfers between devices: 6.45 us -> 0.96 us
  Pallas kernels: 11.9 us -> 10.4 us
    all_to_all x0 -> x1, blocking collectives: none -> 16.2 us  [on_device(): lax.all_to_all(message, 'box', split_axis=0, concat_axis=0, tiled=True)]
    all_to_all x1 -> x0, starting transfers between devices: 8.82 us -> none  [on_device(): lax.all_to_all(message, 'box', split_axis=0, concat_axis=0, tiled=True)]
    all_to_all x1 -> x0, waiting for transfers between devices: 6.43 us -> none  [on_device(): lax.all_to_all(message, 'box', split_axis=0, concat_axis=0, tiled=True)]
    ppermute x4, starting transfers between devices: 11.4 us -> 9.75 us  [swap(): lax.ppermute(value, 'term', [(i, other(i) % terms) for i in range(terms)])]
    pallas_call x7 -> x6, Pallas kernels: 11.9 us -> 10.4 us  [call(): pl.pallas_call(kernel, out_shape=outs, in_specs=[vmem] * len(args), out_s...]
    ppermute x4, waiting for transfers between devices: 0.01 us -> 0.96 us  [swap(): lax.ppermute(value, 'term', [(i, other(i) % terms) for i in range(terms)])]
  transfers between devices with their start and end apart: 6 -> 5, of which waited for: 1 -> 1; matrix products, arithmetic and copies ran while one was open for 0% -> 0% of each run, Pallas kernels for 20% -> 18%
where the time goes in v2:
time: 45.7 us; the launch traced here: 45.4 us
  starting transfers between devices  17.8 us (39%)
  blocking collectives  16.2 us (35%)
  Pallas kernels  10.4 us (23%)
  waiting for transfers between devices  0.96 us (2%)
    all_to_all x1, blocking collectives, on_device(): lax.all_to_all(message, 'box', split_axis=0, concat_axis=0, tiled=True)  16.2 us
    pallas_call x6, Pallas kernels, call(): pl.pallas_call(kernel, out_shape=outs, in_specs=[vmem] * len(args), out_s...  10.4 us
    ppermute x4, starting transfers between devices, swap(): lax.ppermute(value, 'term', [(i, other(i) % terms) for i in range(terms)])  9.75 us
    all_to_all x1, starting transfers between devices, on_device(): lax.all_to_all(keys, 'box', split_axis=0, concat_axis=0, tiled=True)  8.04 us
    ppermute x4, waiting for transfers between devices, swap(): lax.ppermute(value, 'term', [(i, other(i) % terms) for i in range(terms)])  0.96 us
  transfers between devices with their start and end apart: 5, of which 1 were waited for; matrix products, arithmetic and copies ran while one was open for 0% of the time, Pallas kernels for 18%

profile of v2, /device:TPU:1, one launch (start us, length us, event | category | flops | bytes accessed | tf_op | source)
XLA Modules:
  0.0 45.4 jit_solution(7656307172599473415)
XLA Ops:
  0.0 0.0 copy-start
  0.0 7.7 %collective-permute-start = (bf16[96,16]{1,0:T(8,128)(2,1)}, bf16[96,16]{1,0:T(8,128)(2,1)S(1)}, u32[]{:S(2)}, u32[]{:S(2)}) collective-permute-start(bf16[96,16]{1,0:T(8,128)(2,1)} %bitcast.10), channel_id=1, source_target_pairs={{0,4},{1,5},{2,6},{3,7},{4,0},{5,1},{6,2},{7,3},{8,12},{9,13},{10,... | collective-permute-start | bytes 9224 | tf_op jit(solution)/shard_map/ppermute | solution.py:225
  7.7 1.7 %shard_map.37 = (s32[32,128]{1,0:T(8,128)}, bf16[96,16]{1,0:T(8,128)(2,1)S(1)}) custom-call(s32[16,13]{1,0:T(8,128)} %neighbors_ref.3, bf16[96,16]{1,0:T(8,128)(2,1)} %bitcast.11), custom_call_target="tpu_custom_call" | custom-call | tf_op jit(solution)/shard_map/pallas_call | solution.py:202
  9.4 8.0 %all-to-all-start = ((s32[32,1,128]{2,1,0:T(1,128)}), s32[32,1,128]{2,1,0:T(1,128)S(1)}, u32[]{:S(2)}, u32[]{:S(2)}) async-start(s32[32,1,128]{2,1,0:T(1,128)} %bitcast.2), calls=%async_computation | async-start | bytes 32768 | tf_op jit(solution)/shard_map/all_to_all | solution.py:257
  17.4 0.0 collective-permute-done
  17.5 0.8 %collective-permute-start.3 = (bf16[192,16]{1,0:T(8,128)(2,1)S(1)}, bf16[192,16]{1,0:T(8,128)(2,1)S(1)}, u32[]{:S(2)}, u32[]{:S(2)}) collective-permute-start(bf16[192,16]{1,0:T(8,128)(2,1)S(1)} %constant_dynamic-update-slice_fusion.refs_0_), channel_id=1, source_target_pairs={{0,1},{1,0},{2,3},{3,2},{4,5},{5,4},{6,7},{7,6},{8,9},{9,8},{10,11... | collective-permute-start | bytes 18440 | tf_op jit(solution)/shard_map/ppermute | solution.py:225
  18.3 1.2 %collective-permute-start.1 = (bf16[192,16]{1,0:T(8,128)(2,1)S(1)}, bf16[192,16]{1,0:T(8,128)(2,1)S(1)}, u32[]{:S(2)}, u32[]{:S(2)}) collective-permute-start(bf16[192,16]{1,0:T(8,128)(2,1)S(1)} %constant_dynamic-update-slice_fusion.refs_0_), channel_id=1, source_target_pairs={{0,2},{1,3},{2,0},{3,1},{4,6},{5,7},{6,4},{7,5},{8,10},{9,11},{10,... | collective-permute-start | bytes 18440 | tf_op jit(solution)/shard_map/ppermute | solution.py:225
  19.5 0.0 collective-permute-start.2
  19.5 0.0 copy-done
  19.5 1.7 %shard_map.38.refs_1_ = f32[9,96,256]{2,1,0:T(8,128)S(1)} custom-call(bf16[256,256]{1,0:T(8,128)(2,1)S(1)} %bitcast.6, bf16[192,16]{1,0:T(8,128)(2,1)S(1)} %constant_dynamic-update-slice_fusion.refs_0_), custom_call_target="tpu_custom_call" | custom-call | tf_op jit(solution)/shard_map/pallas_call | solution.py:202
  21.2 0.0 collective-permute-done.3.refs_0_
  21.2 1.7 %shard_map.39.refs_2_ = f32[9,96,256]{2,1,0:T(8,128)S(1)} custom-call(bf16[256,256]{1,0:T(8,128)(2,1)S(1)} %bitcast.7, bf16[192,16]{1,0:T(8,128)(2,1)S(1)} %collective-permute-done.3.refs_0_, f32[9,96,256]{2,1,0:T(8,128)S(1)} %shard_map.38.refs_1_), custom_call_target="tpu_custom_call" | custom-call | tf_op jit(solution)/shard_map/pallas_call | solution.py:202
  23.0 0.0 collective-permute-done.1.refs_0_
  23.0 0.9 %collective-permute-done.2.refs_1_ = bf16[192,16]{1,0:T(8,128)(2,1)S(1)} collective-permute-done((bf16[192,16]{1,0:T(8,128)(2,1)S(1)}, bf16[192,16]{1,0:T(8,128)(2,1)S(1)}, u32[]{:S(2)}, u32[]{:S(2)}) %collective-permute-start.2) | collective-permute-done | bytes 6176 | tf_op jit(solution)/shard_map/ppermute | solution.py:225
  23.9 0.0 copy-start.1
  23.9 3.1 %shard_map.40 = (bf16[432,512]{1,0:T(8,128)(2,1)S(1)}, bf16[432,512]{1,0:T(8,128)(2,1)S(1)}) custom-call(bf16[256,256]{1,0:T(8,128)(2,1)S(1)} %bitcast.8, bf16[192,16]{1,0:T(8,128)(2,1)S(1)} %collective-permute-done.1.refs_0_, bf16[192,16]{1,0:T(8,128)(2,1)S(1)} %collective-permute-done.2.refs_1_, f32[9,96,256]{2,1,0:T(8,128)S(1)} %shard_map.39.refs_2_), custom_call_target="tpu_custom_call" | custom-call | tf_op jit(solution)/shard_map/pallas_call | solution.py:202
  27.0 0.0 all-to-all-done
  27.0 0.0 copy-done.1
  27.0 1.4 %shard_map.41 = (bf16[32,16,128]{2,1,0:T(8,128)(2,1)S(1)}, f32[64,128]{1,0:T(8,128)S(1)}, bf16[64,512]{1,0:T(8,128)(2,1)S(1)}) custom-call(s32[32,128]{1,0:T(8,128)} %get-tuple-element.12.keys_ref, s32[32,128]{1,0:T(8,128)S(1)} %bitcast.9, s32[16,13]{1,0:T(8,128)S(1)} %copy-done.1, bf16[432,512]{1,0:T(8,128)(2,1)S(1)} %get-tuple-element.14.high_ref, ...), custom_call_target="tpu_custom_call" | custom-call | tf_op jit(solution)/shard_map/pallas_call | solution.py:202
  28.5 16.2 %all_to_all.16.arrived_ref = bf16[32,16,128]{2,1,0:T(8,128)(2,1)S(1)} all-to-all(bf16[32,16,128]{2,1,0:T(8,128)(2,1)S(1)} %get-tuple-element.18), channel_id=1, replica_groups=mesh['box'=32,'term'=8] {'box'}, dimensions={0} | all-to-all | bytes 262144 | tf_op jit(solution)/shard_map/all_to_all | solution.py:279
  44.7 0.8 %shard_map.42 = f32[2,16,256]{2,1,0:T(8,128)} custom-call(f32[64,128]{1,0:T(8,128)S(1)} %get-tuple-element.16.local_ref, bf16[64,512]{1,0:T(8,128)(2,1)S(1)} %get-tuple-element.17.place_ref, bf16[32,16,128]{2,1,0:T(8,128)(2,1)S(1)} %all_to_all.16.arrived_ref), custom_call_target="tpu_custom_call" | custom-call | tf_op jit(solution)/shard_map/pallas_call | solution.py:202
  (2 shorter events, 0.0 us)
Async XLA Ops:
  0.0 19.5 %copy-start = (bf16[16,16,256]{2,1,0:T(8,128)(2,1)S(1)}, bf16[16,16,256]{2,1,0:T(8,128)(2,1)}, u32[]{:S(2)}) copy-start(bf16[16,16,256]{2,1,0:T(8,128)(2,1)} %param.3) | copy-start | bytes 393220
  0.0 17.4 %collective-permute-start = (bf16[96,16]{1,0:T(8,128)(2,1)}, bf16[96,16]{1,0:T(8,128)(2,1)S(1)}, u32[]{:S(2)}, u32[]{:S(2)}) collective-permute-start(bf16[96,16]{1,0:T(8,128)(2,1)} %bitcast.10), channel_id=1, source_target_pairs={{0,4},{1,5},{2,6},{3,7},{4,0},{5,1},{6,2},{7,3},{8,12},{9,13},{10,... | collective-permute-start | bytes 9224 | tf_op jit(solution)/shard_map/ppermute | solution.py:225
  9.4 17.6 %all-to-all-start = ((s32[32,1,128]{2,1,0:T(1,128)}), s32[32,1,128]{2,1,0:T(1,128)S(1)}, u32[]{:S(2)}, u32[]{:S(2)}) async-start(s32[32,1,128]{2,1,0:T(1,128)} %bitcast.2), calls=%async_computation | async-start | bytes 32768 | tf_op jit(solution)/shard_map/all_to_all | solution.py:257
  17.5 3.8 %collective-permute-start.3 = (bf16[192,16]{1,0:T(8,128)(2,1)S(1)}, bf16[192,16]{1,0:T(8,128)(2,1)S(1)}, u32[]{:S(2)}, u32[]{:S(2)}) collective-permute-start(bf16[192,16]{1,0:T(8,128)(2,1)S(1)} %constant_dynamic-update-slice_fusion.refs_0_), channel_id=1, source_target_pairs={{0,1},{1,0},{2,3},{3,2},{4,5},{5,4},{6,7},{7,6},{8,9},{9,8},{10,11... | collective-permute-start | bytes 18440 | tf_op jit(solution)/shard_map/ppermute | solution.py:225
  18.3 4.7 %collective-permute-start.1 = (bf16[192,16]{1,0:T(8,128)(2,1)S(1)}, bf16[192,16]{1,0:T(8,128)(2,1)S(1)}, u32[]{:S(2)}, u32[]{:S(2)}) collective-permute-start(bf16[192,16]{1,0:T(8,128)(2,1)S(1)} %constant_dynamic-update-slice_fusion.refs_0_), channel_id=1, source_target_pairs={{0,2},{1,3},{2,0},{3,1},{4,6},{5,7},{6,4},{7,5},{8,10},{9,11},{10,... | collective-permute-start | bytes 18440 | tf_op jit(solution)/shard_map/ppermute | solution.py:225
  19.5 4.4 %collective-permute-start.2 = (bf16[192,16]{1,0:T(8,128)(2,1)S(1)}, bf16[192,16]{1,0:T(8,128)(2,1)S(1)}, u32[]{:S(2)}, u32[]{:S(2)}) collective-permute-start(bf16[192,16]{1,0:T(8,128)(2,1)S(1)} %constant_dynamic-update-slice_fusion.refs_0_), channel_id=1, source_target_pairs={{0,7},{1,2},{2,1},{3,4},{4,3},{5,6},{6,5},{7,0},{8,15},{9,10},{10,... | collective-permute-start | bytes 18440 | tf_op jit(solution)/shard_map/ppermute | solution.py:225
  23.9 3.1 %copy-start.1 = (s32[16,13]{1,0:T(8,128)S(1)}, s32[16,13]{1,0:T(8,128)}, u32[]{:S(2)}) copy-start(s32[16,13]{1,0:T(8,128)} %neighbors_ref.3) | copy-start | bytes 2500

commit v3 on v2

--- a/solution.py
+++ b/solution.py
@@ -16,8 +16,34 @@
     return lax.broadcasted_iota(jnp.int32, shape, axis)
 
 
-def request_kernel(neighbors_ref, operators_ref, keys_ref, mine_ref):
-    mine_ref[...] = operators_ref[...]
+def request_kernel(
+    neighbors_hbm,
+    operators_hbm,
+    coeffs_hbm,
+    keys_ref,
+    mine_ref,
+    near_ref,
+    neighbors_ref,
+    operators_ref,
+    arrivals,
+):
+    fetches = [
+        pltpu.make_async_copy(source, target, arrivals.at[i])
+        for i, (source, target) in enumerate(
+            (
+                (neighbors_hbm, neighbors_ref),
+                (operators_hbm, operators_ref),
+                (coeffs_hbm, near_ref),
+            )
+        )
+    ]
+    for fetch in fetches:
+        fetch.start()
+    fetches[1].wait()
+    blocks = [operators_ref[16 * i : 16 * (i + 1), :] for i in range(6)]
+    pad = jnp.zeros((16, 32), operators_ref.dtype)
+    mine_ref[0] = jnp.concatenate(blocks + [pad], axis=1)
+    fetches[0].wait()
     box_count, column_count = neighbors_ref.shape
     groups = keys_ref.shape[0]
     myself = lax.axis_index("box").astype(jnp.int32)
@@ -39,6 +65,7 @@
     first = jnp.where(first == BIG, -1, first)
     lane = iota(keys_ref.shape, 1)
     keys_ref[...] = jnp.where(lane == 0, first, jnp.where(lane == 1, last, -1))
+    fetches[2].wait()
 
 
 def image_kernel(terms, pieces, first, final, coeffs_ref, *refs):
@@ -53,7 +80,12 @@
     row = iota((16, 256), 0)
     to_outer = jnp.where((lane >> 4) == row, 1.0, 0.0).astype(jnp.bfloat16)
     to_inner = jnp.where((lane & 15) == row, 1.0, 0.0).astype(jnp.bfloat16)
-    rows = jnp.concatenate([ref[...] for ref in rows_refs], axis=0)
+    blocks = []
+    for ref in rows_refs:
+        for i in range(ref.shape[0]):
+            packed = ref[i]
+            blocks += [packed[:, 16 * b : 16 * (b + 1)] for b in range(6)]
+    rows = jnp.concatenate(blocks, axis=0)
     outer_ref[...] = jnp.dot(rows, to_outer, preferred_element_type=jnp.float32)
     inner_ref[...] = jnp.dot(rows, to_inner, preferred_element_type=jnp.float32).astype(
         jnp.bfloat16
@@ -111,6 +143,19 @@
                         low_ref[to] = low[at : at + 16, :]
 
 
+def flip_of(groups):
+    return groups // 2 + groups // 8
+
+
+def flipped(rows):
+    groups = rows.shape[0]
+    part = groups // 8
+    flip = flip_of(groups) // part
+    return jnp.concatenate(
+        [rows[part * (i ^ flip) : part * ((i ^ flip) + 1), :] for i in range(8)], axis=0
+    )
+
+
 def message_kernel(
     keys_ref,
     guests_ref,
@@ -122,13 +167,15 @@
     place_ref,
     chunk_ref,
 ):
+    keys = flipped(keys_ref[...])
+    guests = flipped(guests_ref[...])
     spots = []
     for slot in range(CAP):
-        key = keys_ref[:, slot : slot + 1]
+        key = keys[:, slot : slot + 1]
         spot = (12 - ((key >> 8) & 15)) * 16 + ((key >> 4) & 15)
         spots.append(jnp.where(key < 0, -1, spot))
     for slot in range(CAP):
-        key = guests_ref[:, slot : slot + 1]
+        key = guests[:, slot : slot + 1]
         spot = (14 + ((key >> 8) & 15)) * 16 + (key & 15)
         spots.append(jnp.where(key < 0, -1, spot))
     lane = iota((32, 432), 1)
@@ -166,8 +213,7 @@
     for part in range(4):
         local_ref[16 * part : 16 * (part + 1), :] = local[:, 128 * part : 128 * (part + 1)]
     lane = iota((32, 128), 1)
-    guests = guests_ref[...]
-    keys = jnp.where((lane == 2) | (lane == 3), jnp.roll(keys_ref[...], 2, axis=1), -1)
+    keys = jnp.where((lane == 2) | (lane == 3), jnp.roll(keys, 2, axis=1), -1)
     target = jnp.where(lane < 2, guests & 15, (keys >> 4) & 15)
     target = jnp.where(jnp.where(lane < 2, guests, keys) < 0, -1, target)
     spread = jnp.where((iota((32, 512), 1) >> 4) == iota((32, 512), 0), 1.0, 0.0)
@@ -197,12 +243,12 @@
         ]
 
 
-def call(kernel, outs, scratch, *args):
+def call(kernel, outs, scratch, *args, place=pltpu.VMEM):
     vmem = pl.BlockSpec(memory_space=pltpu.VMEM)
     return pl.pallas_call(
         kernel,
         out_shape=outs,
-        in_specs=[vmem] * len(args),
+        in_specs=[pl.BlockSpec(memory_space=place)] * len(args),
         out_specs=jax.tree.map(lambda _: vmem, outs),
         scratch_shapes=scratch,
     )(*args)
@@ -217,7 +263,7 @@
     groups = lax.axis_size("box")
     terms = lax.axis_size("term")
     shape = pltpu.VMEM
-    coeffs = near(coeffs.reshape(degree * box_count, plane_size))
+    coeffs = coeffs.reshape(degree * box_count, plane_size)
     totals = shape((9, 6 * box_count, plane_size), jnp.float32)
     image = shape((27 * box_count, 2 * plane_size), jnp.bfloat16)
 
@@ -225,7 +271,7 @@
         return lax.ppermute(value, "term", [(i, other(i) % terms) for i in range(terms)])
 
     def images(rows, before, final):
-        height = sum(piece.shape[0] for piece in rows)
+        height = 6 * degree * sum(piece.shape[0] for piece in rows)
         count = height // (3 * degree)
         scratch = [
             pltpu.VMEM((height, plane_size), jnp.float32),
@@ -240,28 +286,36 @@
             functools.partial(image_kernel, count, len(rows), before is None, final),
             (image, image) if final else totals,
             scratch,
-            coeffs,
+            near(coeffs),
             *[near(piece) for piece in rows],
             *([] if before is None else [near(before)]),
         )
 
-    mine = operators.reshape(-1, degree)
-    other = swap(mine, lambda i: i ^ 4)
-    keys, pair = call(
+    keys, mine, coeffs = call(
         request_kernel,
-        (shape((groups, 128), jnp.int32), shape(mine.shape, mine.dtype)),
-        [],
+        (
+            shape((groups, 128), jnp.int32),
+            shape((1, degree, 128), operators.dtype),
+            shape(coeffs.shape, coeffs.dtype),
+        ),
+        [
+            pltpu.VMEM(neighbors.shape, neighbors.dtype),
+            pltpu.VMEM((6 * degree, degree), operators.dtype),
+            pltpu.SemaphoreType.DMA((3,)),
+        ],
         neighbors,
-        mine,
-    )
+        operators.reshape(-1, degree),
+        coeffs,
+        place=pl.ANY,
+    )
+    pieces = [mine]
+    for bit in (1, 2, 3):
+        pieces.append(swap(mine, functools.partial(lambda bit, i: i ^ bit, bit)))
     guests = lax.all_to_all(keys, "box", split_axis=0, concat_axis=0, tiled=True)
-    pair = jnp.concatenate([pair, other], axis=0)
-    ones = swap(pair, lambda i: i ^ 1)
-    twos = swap(pair, lambda i: i ^ 2)
-    threes = swap(pair, lambda i: i + (1 if i % 2 else -1))
-    total = images([pair], None, False)
-    total = images([ones], total, False)
-    high, low = images([twos, threes], total, True)
+    quad = jnp.concatenate(pieces, axis=0)
+    rest = swap(quad, lambda i: i ^ 6)
+    total = images([quad], None, False)
+    high, low = images([rest], total, True)
     message, local, place = call(
         message_kernel,
         (
@@ -276,7 +330,10 @@
         near(high),
         near(low),
     )
-    arrived = lax.all_to_all(message, "box", split_axis=0, concat_axis=0, tiled=True)
+    ranks = [i ^ flip_of(groups) for i in range(groups)]
+    arrived = lax.all_to_all(
+        message, "box", split_axis=0, concat_axis=0, tiled=True, axis_index_groups=[ranks]
+    )
     return call(
         gather_kernel,
         jax.ShapeDtypeStruct((2, box_count, plane_size), jnp.float32),

time: 45.7 us -> 43.1 us (0.943)
  blocking collectives: 16.2 us -> 10.8 us
  waiting for transfers between devices: 0.96 us -> 4.86 us
  starting transfers between devices: 17.8 us -> 16.8 us
    all_to_all x1, blocking collectives: 16.2 us -> 10.8 us  [on_device(): lax.all_to_all(message, 'box', split_axis=0, concat_axis=0, tiled=True, a...]
    ppermute x4, waiting for transfers between devices: 0.96 us -> 4.23 us  [swap(): lax.ppermute(value, 'term', [(i, other(i) % terms) for i in range(terms)])]
    ppermute x4, starting transfers between devices: 9.75 us -> 7.04 us  [swap(): lax.ppermute(value, 'term', [(i, other(i) % terms) for i in range(terms)])]
    all_to_all x1, starting transfers between devices: 8.04 us -> 9.75 us  [on_device(): lax.all_to_all(keys, 'box', split_axis=0, concat_axis=0, tiled=True)]
    all_to_all x1, waiting for transfers between devices: 0.01 us -> 0.63 us  [on_device(): lax.all_to_all(keys, 'box', split_axis=0, concat_axis=0, tiled=True)]
    pallas_call x6 -> x5, Pallas kernels: 10.4 us -> 10.2 us  [call(): pl.pallas_call(kernel, out_shape=outs, in_specs=[pl.BlockSpec(memory_spac...]
  transfers between devices with their start and end apart: 5 -> 5, of which waited for: 1 -> 3; matrix products, arithmetic and copies ran while one was open for 0% -> 0% of each run, Pallas kernels for 18% -> 15%
where the time goes in v3:
time: 43.1 us; the launch traced here: 42.7 us
  starting transfers between devices  16.8 us (39%)
  blocking collectives  10.8 us (25%)
  Pallas kernels  10.2 us (24%)
  waiting for transfers between devices  4.86 us (11%)
    all_to_all x1, blocking collectives, on_device(): lax.all_to_all(message, 'box', split_axis=0, concat_axis=0, tiled=True, a...  10.8 us
    pallas_call x5, Pallas kernels, call(): pl.pallas_call(kernel, out_shape=outs, in_specs=[pl.BlockSpec(memory_spac...  10.2 us
    all_to_all x1, starting transfers between devices, on_device(): lax.all_to_all(keys, 'box', split_axis=0, concat_axis=0, tiled=True)  9.75 us
    ppermute x4, starting transfers between devices, swap(): lax.ppermute(value, 'term', [(i, other(i) % terms) for i in range(terms)])  7.04 us
    ppermute x4, waiting for transfers between devices, swap(): lax.ppermute(value, 'term', [(i, other(i) % terms) for i in range(terms)])  4.23 us
  transfers between devices with their start and end apart: 5, of which 3 were waited for; matrix products, arithmetic and copies ran while one was open for 0% of the time, Pallas kernels for 15%

profile of v3, /device:TPU:1, one launch (start us, length us, event | category | flops | bytes accessed | tf_op | source)
XLA Modules:
  0.0 42.7 jit_solution(7081973371800155643)
XLA Ops:
  0.0 1.7 %shard_map.37 = (s32[32,128]{1,0:T(8,128)}, bf16[1,16,128]{2,1,0:T(8,128)(2,1)S(1)}, bf16[256,256]{1,0:T(8,128)(2,1)S(1)}) custom-call(s32[16,13]{1,0:T(8,128)} %neighbors_ref.1, bf16[96,16]{1,0:T(8,128)(2,1)} %bitcast.8, bf16[256,256]{1,0:T(8,128)(2,1)} %bitcast.7), custom_call_target="tpu_custom_call" | custom-call | tf_op jit(solution)/shard_map/pallas_call | solution.py:248
  1.7 2.5 %collective-permute-start = (bf16[1,16,128]{2,1,0:T(8,128)(2,1)S(1)}, bf16[1,16,128]{2,1,0:T(8,128)(2,1)S(1)}, u32[]{:S(2)}, u32[]{:S(2)}) collective-permute-start(bf16[1,16,128]{2,1,0:T(8,128)(2,1)S(1)} %get-tuple-element.15), channel_id=1, source_target_pairs={{0,1},{1,0},{2,3},{3,2},{4,5},{5,4},{6,7},{7,6},{8,9},{9,8},{10,11... | collective-permute-start | bytes 12296 | tf_op jit(solution)/shard_map/ppermute | solution.py:271
  4.3 3.0 %collective-permute-start.1 = (bf16[1,16,128]{2,1,0:T(8,128)(2,1)S(1)}, bf16[1,16,128]{2,1,0:T(8,128)(2,1)S(1)}, u32[]{:S(2)}, u32[]{:S(2)}) collective-permute-start(bf16[1,16,128]{2,1,0:T(8,128)(2,1)S(1)} %get-tuple-element.15), channel_id=1, source_target_pairs={{0,2},{1,3},{2,0},{3,1},{4,6},{5,7},{6,4},{7,5},{8,10},{9,11},{10,... | collective-permute-start | bytes 12296 | tf_op jit(solution)/shard_map/ppermute | solution.py:271
  7.3 0.0 collective-permute-start.2
  7.3 0.0 collective-permute-done
  7.3 1.0 %collective-permute-done.1 = bf16[1,16,128]{2,1,0:T(8,128)(2,1)S(1)} collective-permute-done((bf16[1,16,128]{2,1,0:T(8,128)(2,1)S(1)}, bf16[1,16,128]{2,1,0:T(8,128)(2,1)S(1)}, u32[]{:S(2)}, u32[]{:S(2)}) %collective-permute-start.1) | collective-permute-done | bytes 4128 | tf_op jit(solution)/shard_map/ppermute | solution.py:271
  8.3 3.3 %collective-permute-done.2 = bf16[1,16,128]{2,1,0:T(8,128)(2,1)S(1)} collective-permute-done((bf16[1,16,128]{2,1,0:T(8,128)(2,1)S(1)}, bf16[1,16,128]{2,1,0:T(8,128)(2,1)S(1)}, u32[]{:S(2)}, u32[]{:S(2)}) %collective-permute-start.2) | collective-permute-done | bytes 4128 | tf_op jit(solution)/shard_map/ppermute | solution.py:271
  11.5 1.5 %collective-permute-start.3 = (bf16[4,16,128]{2,1,0:T(8,128)(2,1)S(1)}, bf16[4,16,128]{2,1,0:T(8,128)(2,1)S(1)}, u32[]{:S(2)}, u32[]{:S(2)}) collective-permute-start(bf16[4,16,128]{2,1,0:T(8,128)(2,1)S(1)} %constant_dynamic-update-slice_fusion.refs_0_), channel_id=1, source_target_pairs={{0,6},{1,7},{2,4},{3,5},{4,2},{5,3},{6,0},{7,1},{8,14},{9,15},{10,... | collective-permute-start | bytes 49160 | tf_op jit(solution)/shard_map/ppermute | solution.py:271
  13.0 9.7 %all-to-all-start = ((s32[32,1,128]{2,1,0:T(1,128)}), s32[32,1,128]{2,1,0:T(1,128)S(1)}, u32[]{:S(2)}, u32[]{:S(2)}) async-start(s32[32,1,128]{2,1,0:T(1,128)} %bitcast.3), calls=%async_computation | async-start | bytes 32768 | tf_op jit(solution)/shard_map/all_to_all | solution.py:314
  22.8 3.1 %shard_map.38.refs_1_ = f32[9,96,256]{2,1,0:T(8,128)S(1)} custom-call(bf16[256,256]{1,0:T(8,128)(2,1)S(1)} %get-tuple-element.14.coeffs_ref, bf16[4,16,128]{2,1,0:T(8,128)(2,1)S(1)} %constant_dynamic-update-slice_fusion.refs_0_), custom_call_target="tpu_custom_call" | custom-call | tf_op jit(solution)/shard_map/pallas_call | solution.py:248
  25.9 0.0 collective-permute-done.3.refs_0_
  25.9 0.0 copy-start
  25.9 3.1 %shard_map.39 = (bf16[432,512]{1,0:T(8,128)(2,1)S(1)}, bf16[432,512]{1,0:T(8,128)(2,1)S(1)}) custom-call(bf16[256,256]{1,0:T(8,128)(2,1)S(1)} %get-tuple-element.14.coeffs_ref, bf16[4,16,128]{2,1,0:T(8,128)(2,1)S(1)} %collective-permute-done.3.refs_0_, f32[9,96,256]{2,1,0:T(8,128)S(1)} %shard_map.38.refs_1_), custom_call_target="tpu_custom_call" | custom-call | tf_op jit(solution)/shard_map/pallas_call | solution.py:248
  29.1 0.6 %all-to-all-done = s32[32,1,128]{2,1,0:T(1,128)S(1)} async-done(((s32[32,1,128]{2,1,0:T(1,128)}), s32[32,1,128]{2,1,0:T(1,128)S(1)}, u32[]{:S(2)}, u32[]{:S(2)}) %all-to-all-start) | async-done | bytes 16416 | tf_op jit(solution)/shard_map/all_to_all | solution.py:314
  29.7 0.0 copy-done
  29.7 1.4 %shard_map.40 = (bf16[32,16,128]{2,1,0:T(8,128)(2,1)S(1)}, f32[64,128]{1,0:T(8,128)S(1)}, bf16[64,512]{1,0:T(8,128)(2,1)S(1)}) custom-call(s32[32,128]{1,0:T(8,128)} %get-tuple-element.13.keys_ref, s32[32,128]{1,0:T(8,128)S(1)} %bitcast.6, s32[16,13]{1,0:T(8,128)S(1)} %copy-done, bf16[432,512]{1,0:T(8,128)(2,1)S(1)} %get-tuple-element.16.high_ref, ...), custom_call_target="tpu_custom_call" | custom-call | tf_op jit(solution)/shard_map/pallas_call | solution.py:248
  31.1 10.8 %all_to_all.16.arrived_ref = bf16[32,16,128]{2,1,0:T(8,128)(2,1)S(1)} all-to-all(bf16[32,16,128]{2,1,0:T(8,128)(2,1)S(1)} %get-tuple-element.20), channel_id=1, replica_groups={{160,168,176,184,128,136,144,152,224,232,240,248,192,200,208,216,32,40,..., dimensions={0} | all-to-all | bytes 262144 | tf_op jit(solution)/shard_map/all_to_all | solution.py:334
  41.9 0.8 %shard_map.41 = f32[2,16,256]{2,1,0:T(8,128)} custom-call(f32[64,128]{1,0:T(8,128)S(1)} %get-tuple-element.18.local_ref, bf16[64,512]{1,0:T(8,128)(2,1)S(1)} %get-tuple-element.19.place_ref, bf16[32,16,128]{2,1,0:T(8,128)(2,1)S(1)} %all_to_all.16.arrived_ref), custom_call_target="tpu_custom_call" | custom-call | tf_op jit(solution)/shard_map/pallas_call | solution.py:248
  (4 shorter events, 0.0 us)
Async XLA Ops:
  1.7 5.5 %collective-permute-start = (bf16[1,16,128]{2,1,0:T(8,128)(2,1)S(1)}, bf16[1,16,128]{2,1,0:T(8,128)(2,1)S(1)}, u32[]{:S(2)}, u32[]{:S(2)}) collective-permute-start(bf16[1,16,128]{2,1,0:T(8,128)(2,1)S(1)} %get-tuple-element.15), channel_id=1, source_target_pairs={{0,1},{1,0},{2,3},{3,2},{4,5},{5,4},{6,7},{7,6},{8,9},{9,8},{10,11... | collective-permute-start | bytes 12296 | tf_op jit(solution)/shard_map/ppermute | solution.py:271
  4.3 4.0 %collective-permute-start.1 = (bf16[1,16,128]{2,1,0:T(8,128)(2,1)S(1)}, bf16[1,16,128]{2,1,0:T(8,128)(2,1)S(1)}, u32[]{:S(2)}, u32[]{:S(2)}) collective-permute-start(bf16[1,16,128]{2,1,0:T(8,128)(2,1)S(1)} %get-tuple-element.15), channel_id=1, source_target_pairs={{0,2},{1,3},{2,0},{3,1},{4,6},{5,7},{6,4},{7,5},{8,10},{9,11},{10,... | collective-permute-start | bytes 12296 | tf_op jit(solution)/shard_map/ppermute | solution.py:271
  7.3 4.3 %collective-permute-start.2 = (bf16[1,16,128]{2,1,0:T(8,128)(2,1)S(1)}, bf16[1,16,128]{2,1,0:T(8,128)(2,1)S(1)}, u32[]{:S(2)}, u32[]{:S(2)}) collective-permute-start(bf16[1,16,128]{2,1,0:T(8,128)(2,1)S(1)} %get-tuple-element.15), channel_id=1, source_target_pairs={{0,3},{1,2},{2,1},{3,0},{4,7},{5,6},{6,5},{7,4},{8,11},{9,10},{10,... | collective-permute-start | bytes 12296 | tf_op jit(solution)/shard_map/ppermute | solution.py:271
  11.5 14.4 %collective-permute-start.3 = (bf16[4,16,128]{2,1,0:T(8,128)(2,1)S(1)}, bf16[4,16,128]{2,1,0:T(8,128)(2,1)S(1)}, u32[]{:S(2)}, u32[]{:S(2)}) collective-permute-start(bf16[4,16,128]{2,1,0:T(8,128)(2,1)S(1)} %constant_dynamic-update-slice_fusion.refs_0_), channel_id=1, source_target_pairs={{0,6},{1,7},{2,4},{3,5},{4,2},{5,3},{6,0},{7,1},{8,14},{9,15},{10,... | collective-permute-start | bytes 49160 | tf_op jit(solution)/shard_map/ppermute | solution.py:271
  13.0 16.6 %all-to-all-start = ((s32[32,1,128]{2,1,0:T(1,128)}), s32[32,1,128]{2,1,0:T(1,128)S(1)}, u32[]{:S(2)}, u32[]{:S(2)}) async-start(s32[32,1,128]{2,1,0:T(1,128)} %bitcast.3), calls=%async_computation | async-start | bytes 32768 | tf_op jit(solution)/shard_map/all_to_all | solution.py:314
  25.9 3.8 %copy-start = (s32[16,13]{1,0:T(8,128)S(1)}, s32[16,13]{1,0:T(8,128)}, u32[]{:S(2)}) copy-start(s32[16,13]{1,0:T(8,128)} %neighbors_ref.1) | copy-start | bytes 2500

commit v4 on v3

--- a/solution.py
+++ b/solution.py
@@ -21,6 +21,7 @@
     operators_hbm,
     coeffs_hbm,
     keys_ref,
+    own_ref,
     mine_ref,
     near_ref,
     neighbors_ref,
@@ -64,7 +65,9 @@
     last = jnp.where(last == first, -1, last)
     first = jnp.where(first == BIG, -1, first)
     lane = iota(keys_ref.shape, 1)
-    keys_ref[...] = jnp.where(lane == 0, first, jnp.where(lane == 1, last, -1))
+    keys = jnp.where(lane == 0, first, jnp.where(lane == 1, last, -1))
+    keys_ref[...] = keys
+    own_ref[...] = keys
     fetches[2].wait()
 
 
@@ -291,9 +294,10 @@
             *([] if before is None else [near(before)]),
         )
 
-    keys, mine, coeffs = call(
+    keys, own, mine, coeffs = call(
         request_kernel,
         (
+            shape((groups, 128), jnp.int32),
             shape((groups, 128), jnp.int32),
             shape((1, degree, 128), operators.dtype),
             shape(coeffs.shape, coeffs.dtype),
@@ -324,7 +328,7 @@
             shape((64, 16 * groups), jnp.bfloat16),
         ),
         [pltpu.VMEM((groups, 16, 128), jnp.float32)],
-        near(keys),
+        near(own),
         near(guests),
         near(neighbors),
         near(high),

time: 43.1 us -> 43.2 us (level)
  starting transfers between devices: 16.8 us -> 19.1 us
  waiting for transfers between devices: 4.86 us -> 3.59 us
  Pallas kernels: 10.2 us -> 9.46 us
    ppermute x4, starting transfers between devices: 7.04 us -> 9.63 us  [swap(): lax.ppermute(value, 'term', [(i, other(i) % terms) for i in range(terms)])]
    ppermute x4, waiting for transfers between devices: 4.23 us -> 2.97 us  [swap(): lax.ppermute(value, 'term', [(i, other(i) % terms) for i in range(terms)])]
    pallas_call x5, Pallas kernels: 10.2 us -> 9.46 us  [call(): pl.pallas_call(kernel, out_shape=outs, in_specs=[pl.BlockSpec(memory_spac...]
where the time goes in v4:
time: 43.2 us; the launch traced here: 43 us
  starting transfers between devices  19.1 us (44%)
  blocking collectives  10.8 us (25%)
  Pallas kernels  9.46 us (22%)
  waiting for transfers between devices  3.59 us (8%)
    all_to_all x1, blocking collectives, on_device(): lax.all_to_all(message, 'box', split_axis=0, concat_axis=0, tiled=True, a...  10.8 us
    ppermute x4, starting transfers between devices, swap(): lax.ppermute(value, 'term', [(i, other(i) % terms) for i in range(terms)])  9.63 us
    pallas_call x5, Pallas kernels, call(): pl.pallas_call(kernel, out_shape=outs, in_specs=[pl.BlockSpec(memory_spac...  9.46 us
    all_to_all x1, starting transfers between devices, on_device(): lax.all_to_all(keys, 'box', split_axis=0, concat_axis=0, tiled=True)  9.45 us
    ppermute x4, waiting for transfers between devices, swap(): lax.ppermute(value, 'term', [(i, other(i) % terms) for i in range(terms)])  2.97 us
  transfers between devices with their start and end apart: 5, of which 3 were waited for; matrix products, arithmetic and copies ran while one was open for 0% of the time, Pallas kernels for 15%

profile of v4, /device:TPU:1, one launch (start us, length us, event | category | flops | bytes accessed | tf_op | source)
XLA Modules:
  0.0 43.0 jit_solution(1624853921154894618)
XLA Ops:
  0.0 1.7 %shard_map.37 = (s32[32,128]{1,0:T(8,128)}, s32[32,128]{1,0:T(8,128)S(1)}, bf16[1,16,128]{2,1,0:T(8,128)(2,1)S(1)}, bf16[256,256]{1,0:T(8,128)(2,1)S(1)}) custom-call(s32[16,13]{1,0:T(8,128)} %neighbors_ref.1, bf16[96,16]{1,0:T(8,128)(2,1)} %bitcast.8, bf16[256,256]{1,0:T(8,128)(2,1)} %bitcast.7), custom_call_target="tpu_custom_call" | custom-call | tf_op jit(solution)/shard_map/pallas_call | solution.py:251
  1.7 5.2 %collective-permute-start.2 = (bf16[1,16,128]{2,1,0:T(8,128)(2,1)S(1)}, bf16[1,16,128]{2,1,0:T(8,128)(2,1)S(1)}, u32[]{:S(2)}, u32[]{:S(2)}) collective-permute-start(bf16[1,16,128]{2,1,0:T(8,128)(2,1)S(1)} %get-tuple-element.17), channel_id=1, source_target_pairs={{0,3},{1,2},{2,1},{3,0},{4,7},{5,6},{6,5},{7,4},{8,11},{9,10},{10,... | collective-permute-start | bytes 12296 | tf_op jit(solution)/shard_map/ppermute | solution.py:274
  7.0 0.0 collective-permute-start.1
  7.0 0.4 collective-permute-start
  7.4 2.4 %collective-permute-done = bf16[1,16,128]{2,1,0:T(8,128)(2,1)S(1)} collective-permute-done((bf16[1,16,128]{2,1,0:T(8,128)(2,1)S(1)}, bf16[1,16,128]{2,1,0:T(8,128)(2,1)S(1)}, u32[]{:S(2)}, u32[]{:S(2)}) %collective-permute-start) | collective-permute-done | bytes 4128 | tf_op jit(solution)/shard_map/ppermute | solution.py:274
  9.8 0.6 %collective-permute-done.1 = bf16[1,16,128]{2,1,0:T(8,128)(2,1)S(1)} collective-permute-done((bf16[1,16,128]{2,1,0:T(8,128)(2,1)S(1)}, bf16[1,16,128]{2,1,0:T(8,128)(2,1)S(1)}, u32[]{:S(2)}, u32[]{:S(2)}) %collective-permute-start.1) | collective-permute-done | bytes 4128 | tf_op jit(solution)/shard_map/ppermute | solution.py:274
  10.4 0.0 collective-permute-done.2
  10.4 4.0 %collective-permute-start.3 = (bf16[4,16,128]{2,1,0:T(8,128)(2,1)S(1)}, bf16[4,16,128]{2,1,0:T(8,128)(2,1)S(1)}, u32[]{:S(2)}, u32[]{:S(2)}) collective-permute-start(bf16[4,16,128]{2,1,0:T(8,128)(2,1)S(1)} %constant_dynamic-update-slice_fusion.refs_0_), channel_id=1, source_target_pairs={{0,6},{1,7},{2,4},{3,5},{4,2},{5,3},{6,0},{7,1},{8,14},{9,15},{10,... | collective-permute-start | bytes 49160 | tf_op jit(solution)/shard_map/ppermute | solution.py:274
  14.4 9.5 %all-to-all-start = ((s32[32,1,128]{2,1,0:T(1,128)}), s32[32,1,128]{2,1,0:T(1,128)S(1)}, u32[]{:S(2)}, u32[]{:S(2)}) async-start(s32[32,1,128]{2,1,0:T(1,128)} %bitcast.3), calls=%async_computation | async-start | bytes 32768 | tf_op jit(solution)/shard_map/all_to_all | solution.py:318
  23.8 3.1 %shard_map.38.refs_1_ = f32[9,96,256]{2,1,0:T(8,128)S(1)} custom-call(bf16[256,256]{1,0:T(8,128)(2,1)S(1)} %get-tuple-element.16.coeffs_ref, bf16[4,16,128]{2,1,0:T(8,128)(2,1)S(1)} %constant_dynamic-update-slice_fusion.refs_0_), custom_call_target="tpu_custom_call" | custom-call | tf_op jit(solution)/shard_map/pallas_call | solution.py:251
  26.9 0.0 collective-permute-done.3.refs_0_
  26.9 0.0 copy-start
  27.0 3.1 %shard_map.39 = (bf16[432,512]{1,0:T(8,128)(2,1)S(1)}, bf16[432,512]{1,0:T(8,128)(2,1)S(1)}) custom-call(bf16[256,256]{1,0:T(8,128)(2,1)S(1)} %get-tuple-element.16.coeffs_ref, bf16[4,16,128]{2,1,0:T(8,128)(2,1)S(1)} %collective-permute-done.3.refs_0_, f32[9,96,256]{2,1,0:T(8,128)S(1)} %shard_map.38.refs_1_), custom_call_target="tpu_custom_call" | custom-call | tf_op jit(solution)/shard_map/pallas_call | solution.py:251
  30.1 0.6 %all-to-all-done = s32[32,1,128]{2,1,0:T(1,128)S(1)} async-done(((s32[32,1,128]{2,1,0:T(1,128)}), s32[32,1,128]{2,1,0:T(1,128)S(1)}, u32[]{:S(2)}, u32[]{:S(2)}) %all-to-all-start) | async-done | bytes 16416 | tf_op jit(solution)/shard_map/all_to_all | solution.py:318
  30.7 0.0 copy-done
  30.7 0.7 %shard_map.40 = (bf16[32,16,128]{2,1,0:T(8,128)(2,1)S(1)}, f32[64,128]{1,0:T(8,128)S(1)}, bf16[64,512]{1,0:T(8,128)(2,1)S(1)}) custom-call(s32[32,128]{1,0:T(8,128)S(1)} %get-tuple-element.14.keys_ref, s32[32,128]{1,0:T(8,128)S(1)} %bitcast.6, s32[16,13]{1,0:T(8,128)S(1)} %copy-done, bf16[432,512]{1,0:T(8,128)(2,1)S(1)} %get-tuple-element.18.high_ref, ...), custom_call_target="tpu_custom_call" | custom-call | tf_op jit(solution)/shard_map/pallas_call | solution.py:251
  31.4 10.8 %all_to_all.16.arrived_ref = bf16[32,16,128]{2,1,0:T(8,128)(2,1)S(1)} all-to-all(bf16[32,16,128]{2,1,0:T(8,128)(2,1)S(1)} %get-tuple-element.22), channel_id=1, replica_groups={{160,168,176,184,128,136,144,152,224,232,240,248,192,200,208,216,32,40,..., dimensions={0} | all-to-all | bytes 262144 | tf_op jit(solution)/shard_map/all_to_all | solution.py:338
  42.2 0.8 %shard_map.41 = f32[2,16,256]{2,1,0:T(8,128)} custom-call(f32[64,128]{1,0:T(8,128)S(1)} %get-tuple-element.20.local_ref, bf16[64,512]{1,0:T(8,128)(2,1)S(1)} %get-tuple-element.21.place_ref, bf16[32,16,128]{2,1,0:T(8,128)(2,1)S(1)} %all_to_all.16.arrived_ref), custom_call_target="tpu_custom_call" | custom-call | tf_op jit(solution)/shard_map/pallas_call | solution.py:251
  (4 shorter events, 0.0 us)
Async XLA Ops:
  1.7 8.6 %collective-permute-start.2 = (bf16[1,16,128]{2,1,0:T(8,128)(2,1)S(1)}, bf16[1,16,128]{2,1,0:T(8,128)(2,1)S(1)}, u32[]{:S(2)}, u32[]{:S(2)}) collective-permute-start(bf16[1,16,128]{2,1,0:T(8,128)(2,1)S(1)} %get-tuple-element.17), channel_id=1, source_target_pairs={{0,3},{1,2},{2,1},{3,0},{4,7},{5,6},{6,5},{7,4},{8,11},{9,10},{10,... | collective-permute-start | bytes 12296 | tf_op jit(solution)/shard_map/ppermute | solution.py:274
  7.0 3.4 %collective-permute-start.1 = (bf16[1,16,128]{2,1,0:T(8,128)(2,1)S(1)}, bf16[1,16,128]{2,1,0:T(8,128)(2,1)S(1)}, u32[]{:S(2)}, u32[]{:S(2)}) collective-permute-start(bf16[1,16,128]{2,1,0:T(8,128)(2,1)S(1)} %get-tuple-element.17), channel_id=1, source_target_pairs={{0,2},{1,3},{2,0},{3,1},{4,6},{5,7},{6,4},{7,5},{8,10},{9,11},{10,... | collective-permute-start | bytes 12296 | tf_op jit(solution)/shard_map/ppermute | solution.py:274
  7.0 2.8 %collective-permute-start = (bf16[1,16,128]{2,1,0:T(8,128)(2,1)S(1)}, bf16[1,16,128]{2,1,0:T(8,128)(2,1)S(1)}, u32[]{:S(2)}, u32[]{:S(2)}) collective-permute-start(bf16[1,16,128]{2,1,0:T(8,128)(2,1)S(1)} %get-tuple-element.17), channel_id=1, source_target_pairs={{0,1},{1,0},{2,3},{3,2},{4,5},{5,4},{6,7},{7,6},{8,9},{9,8},{10,11... | collective-permute-start | bytes 12296 | tf_op jit(solution)/shard_map/ppermute | solution.py:274
  10.4 16.6 %collective-permute-start.3 = (bf16[4,16,128]{2,1,0:T(8,128)(2,1)S(1)}, bf16[4,16,128]{2,1,0:T(8,128)(2,1)S(1)}, u32[]{:S(2)}, u32[]{:S(2)}) collective-permute-start(bf16[4,16,128]{2,1,0:T(8,128)(2,1)S(1)} %constant_dynamic-update-slice_fusion.refs_0_), channel_id=1, source_target_pairs={{0,6},{1,7},{2,4},{3,5},{4,2},{5,3},{6,0},{7,1},{8,14},{9,15},{10,... | collective-permute-start | bytes 49160 | tf_op jit(solution)/shard_map/ppermute | solution.py:274
  14.4 16.4 %all-to-all-start = ((s32[32,1,128]{2,1,0:T(1,128)}), s32[32,1,128]{2,1,0:T(1,128)S(1)}, u32[]{:S(2)}, u32[]{:S(2)}) async-start(s32[32,1,128]{2,1,0:T(1,128)} %bitcast.3), calls=%async_computation | async-start | bytes 32768 | tf_op jit(solution)/shard_map/all_to_all | solution.py:318
  26.9 3.8 %copy-start = (s32[16,13]{1,0:T(8,128)S(1)}, s32[16,13]{1,0:T(8,128)}, u32[]{:S(2)}) copy-start(s32[16,13]{1,0:T(8,128)} %neighbors_ref.1) | copy-start | bytes 2500

commit v5 on v4

--- a/solution.py
+++ b/solution.py
@@ -8,7 +8,6 @@
 from jax.sharding import PartitionSpec as P
 
 CAP = 2
-GROUP = 4
 BIG = 0x7FFFFFFF
 
 
@@ -76,13 +75,13 @@
     before_ref = None if first else refs.pop(0)
     after_ref = None if final else refs.pop(0)
     high_ref, low_ref = (refs.pop(0), refs.pop(0)) if final else (None, None)
-    outer_ref, inner_ref, left_ref, half_ref, kron_ref = refs[:5]
-    sum_ref = refs[5] if final else after_ref
+    outer_ref, inner_ref, left_ref, half_ref, along_ref, across_ref = refs
     term = lax.axis_index("term").astype(jnp.int32)
     lane = iota((16, 256), 1)
     row = iota((16, 256), 0)
     to_outer = jnp.where((lane >> 4) == row, 1.0, 0.0).astype(jnp.bfloat16)
-    to_inner = jnp.where((lane & 15) == row, 1.0, 0.0).astype(jnp.bfloat16)
+    equal = (lane & 15) == row
+    to_inner = jnp.where(equal, 1.0, 0.0).astype(jnp.bfloat16)
     blocks = []
     for ref in rows_refs:
         for i in range(ref.shape[0]):
@@ -90,60 +89,71 @@
             blocks += [packed[:, 16 * b : 16 * (b + 1)] for b in range(6)]
     rows = jnp.concatenate(blocks, axis=0)
     outer_ref[...] = jnp.dot(rows, to_outer, preferred_element_type=jnp.float32)
-    inner_ref[...] = jnp.dot(rows, to_inner, preferred_element_type=jnp.float32).astype(
-        jnp.bfloat16
-    )
-    diagonal = (lane & 15) == row
+    inner_ref[...] = jnp.dot(
+        rows, to_inner[:, :128], preferred_element_type=jnp.float32
+    ).astype(jnp.bfloat16)
     for r in range(terms):
         for m in range(3):
             for al in range(2):
                 line = outer_ref[pl.ds(16 * (3 * r + m) + 2 * term + al, 1), :]
-                block = jnp.where(diagonal, jnp.broadcast_to(line, (16, 256)), 0.0)
+                block = jnp.where(equal, jnp.broadcast_to(line, (16, 256)), 0.0)
                 at = 96 * r + 32 * m + 16 * al
                 left_ref[at : at + 16, :] = block.astype(jnp.bfloat16)
     half = jnp.dot(left_ref[...], coeffs_ref[...], preferred_element_type=jnp.float32)
     half = half.astype(jnp.bfloat16)
     for r in range(terms):
-        half_ref[:, 256 * r : 256 * (r + 1)] = half[96 * r : 96 * (r + 1), :]
-    wide = 256 * GROUP
-    for start in range(0, terms, GROUP):
-        last = start + GROUP == terms
-        for n in range(3):
-            slot = 3 * ((3 * (start // GROUP) + n) % 2)
-            for r in range(start, start + GROUP):
-                to = slice(256 * (r - start), 256 * (r - start + 1))
-                inner = [
-                    inner_ref[16 * (3 * r + p) : 16 * (3 * r + p + 1), :] for p in range(3)
+        for side in range(2):
+            half_ref[r, 96 * side : 96 * (side + 1), :] = half[
+                96 * r : 96 * (r + 1), 128 * side : 128 * (side + 1)
+            ]
+    lane = iota((16, 128), 1)
+    keep = [jnp.where((lane >> 4) == c, 1.0, 0.0).astype(jnp.bfloat16) for c in range(8)]
+    for r in range(terms):
+        matrix = jnp.concatenate(
+            [
+                inner_ref[16 * (3 * r + p) : 16 * (3 * r + p + 1), :] * keep[c]
+                for p in range(3)
+                for c in range(8)
+            ],
+            axis=0,
+        )
+        applied = lax.dot_general(
+            half_ref[r], matrix, (((1,), (1,)), ((), ())), preferred_element_type=jnp.float32
+        ).astype(jnp.bfloat16)
+        for p in range(3):
+            for side in range(2):
+                at = 256 * r + 128 * side
+                along_ref[96 * p : 96 * (p + 1), at : at + 128] = applied[
+                    96 * side : 96 * (side + 1), 128 * p : 128 * (p + 1)
                 ]
-                for a in range(16):
-                    at = 16 * (3 * r + n) + a
-                    line = outer_ref[at : at + 1, :]
-                    line = jnp.broadcast_to(line, (16, 256)).astype(jnp.bfloat16)
-                    for p in range(3):
-                        kron_ref[slot + p, 16 * a : 16 * (a + 1), to] = line * inner[p]
-            for p in range(3):
-                applied = lax.dot_general(
-                    half_ref[:, 256 * start : 256 * start + wide],
-                    kron_ref[slot + p],
-                    (((1,), (1,)), ((), ())),
-                    preferred_element_type=jnp.float32,
-                )
-                if start:
-                    applied = applied + sum_ref[3 * n + p]
-                elif not first:
-                    applied = applied + before_ref[3 * n + p]
-                if not (final and last):
-                    sum_ref[3 * n + p] = applied
-                    continue
-                high = applied.astype(jnp.bfloat16)
-                low = (applied - high.astype(jnp.float32)).astype(jnp.bfloat16)
-                for m in range(3):
-                    code = 9 * m + 3 * n + p
-                    for al in range(2):
-                        at = 32 * m + 16 * al
-                        to = (slice(16 * code, 16 * (code + 1)), slice(256 * al, 256 * (al + 1)))
-                        high_ref[to] = high[at : at + 16, :]
-                        low_ref[to] = low[at : at + 16, :]
+    for n in range(3):
+        for r in range(terms):
+            for a in range(16):
+                at = 16 * (3 * r + n) + a
+                line = outer_ref[at : at + 1, :]
+                line = jnp.broadcast_to(line, (16, 256)).astype(jnp.bfloat16)
+                across_ref[n, 16 * a : 16 * (a + 1), 256 * r : 256 * (r + 1)] = line * to_inner
+        applied = lax.dot_general(
+            along_ref[...],
+            across_ref[n],
+            (((1,), (1,)), ((), ())),
+            preferred_element_type=jnp.float32,
+        )
+        if not first:
+            applied = applied + before_ref[n]
+        if not final:
+            after_ref[n] = applied
+            continue
+        high = applied.astype(jnp.bfloat16)
+        low = (applied - high.astype(jnp.float32)).astype(jnp.bfloat16)
+        for p in range(3):
+            for m in range(3):
+                code = 9 * m + 3 * n + p
+                for al in range(2):
+                    at = 96 * p + 32 * m + 16 * al
+                    to = (slice(16 * code, 16 * (code + 1)), slice(256 * al, 256 * (al + 1)))
+                    high_ref[to] = high[at : at + 16, :]
+                    low_ref[to] = low[at : at + 16, :]
 
 
 def flip_of(groups):
@@ -267,7 +277,7 @@
     terms = lax.axis_size("term")
     shape = pltpu.VMEM
     coeffs = coeffs.reshape(degree * box_count, plane_size)
-    totals = shape((9, 6 * box_count, plane_size), jnp.float32)
+    totals = shape((3, 18 * box_count, plane_size), jnp.float32)
     image = shape((27 * box_count, 2 * plane_size), jnp.bfloat16)
 
     def swap(value, other):
@@ -278,13 +288,12 @@
         count = height // (3 * degree)
         scratch = [
             pltpu.VMEM((height, plane_size), jnp.float32),
-            pltpu.VMEM((height, plane_size), jnp.bfloat16),
+            pltpu.VMEM((height, plane_size // 2), jnp.bfloat16),
             pltpu.VMEM((6 * box_count * count, plane_size), jnp.bfloat16),
-            pltpu.VMEM((6 * box_count, plane_size * count), jnp.bfloat16),
-            pltpu.VMEM((6, plane_size, plane_size * GROUP), jnp.bfloat16),
+            pltpu.VMEM((count, 12 * box_count, plane_size // 2), jnp.bfloat16),
+            pltpu.VMEM((18 * box_count, plane_size * count), jnp.bfloat16),
+            pltpu.VMEM((3, plane_size, plane_size * count), jnp.bfloat16),
         ]
-        if final:
-            scratch.append(pltpu.VMEM((9, 6 * box_count, plane_size), jnp.float32))
         return call(
             functools.partial(image_kernel, count, len(rows), before is None, final),
             (image, image) if final else totals,

time: 43.2 us -> 42.6 us (0.986)
  Pallas kernels: 9.46 us -> 7.07 us
  waiting for transfers between devices: 3.59 us -> 5.98 us
  blocking collectives: 10.8 us -> 10.2 us
    pallas_call x5, Pallas kernels: 9.46 us -> 7.07 us  [call(): pl.pallas_call(kernel, out_shape=outs, in_specs=[pl.BlockSpec(memory_spac...]
    all_to_all x1, waiting for transfers between devices: 0.62 us -> 3.01 us  [on_device(): lax.all_to_all(keys, 'box', split_axis=0, concat_axis=0, tiled=True)]
    all_to_all x1, blocking collectives: 10.8 us -> 10.2 us  [on_device(): lax.all_to_all(message, 'box', split_axis=0, concat_axis=0, tiled=True, a...]
  transfers between devices with their start and end apart: 5 -> 5, of which waited for: 3 -> 3; matrix products, arithmetic and copies ran while one was open for 0% -> 0% of each run, Pallas kernels for 15% -> 9%
where the time goes in v5:
time: 42.6 us; the launch traced here: 42.4 us
  starting transfers between devices  19.1 us (45%)
  blocking collectives  10.2 us (24%)
  Pallas kernels  7.07 us (17%)
  waiting for transfers between devices  5.98 us (14%)
    all_to_all x1, blocking collectives, on_device(): lax.all_to_all(message, 'box', split_axis=0, concat_axis=0, tiled=True, a...  10.2 us
    ppermute x4, starting transfers between devices, swap(): lax.ppermute(value, 'term', [(i, other(i) % terms) for i in range(terms)])  9.63 us
    all_to_all x1, starting transfers between devices, on_device(): lax.all_to_all(keys, 'box', split_axis=0, concat_axis=0, tiled=True)  9.45 us
    pallas_call x5, Pallas kernels, call(): pl.pallas_call(kernel, out_shape=outs, in_specs=[pl.BlockSpec(memory_spac...  7.07 us
    all_to_all x1, waiting for transfers between devices, on_device(): lax.all_to_all(keys, 'box', split_axis=0, concat_axis=0, tiled=True)  3.01 us
    ppermute x4, waiting for transfers between devices, swap(): lax.ppermute(value, 'term', [(i, other(i) % terms) for i in range(terms)])  2.97 us
  transfers between devices with their start and end apart: 5, of which 3 were waited for; matrix products, arithmetic and copies ran while one was open for 0% of the time, Pallas kernels for 9%

profile of v5, /device:TPU:1, one launch (start us, length us, event | category | flops | bytes accessed | tf_op | source)
XLA Modules:
  0.0 42.4 jit_solution(15377200273045360561)
XLA Ops:
  0.0 1.7 %shard_map.37 = (s32[32,128]{1,0:T(8,128)}, s32[32,128]{1,0:T(8,128)S(1)}, bf16[1,16,128]{2,1,0:T(8,128)(2,1)S(1)}, bf16[256,256]{1,0:T(8,128)(2,1)S(1)}) custom-call(s32[16,13]{1,0:T(8,128)} %neighbors_ref.1, bf16[96,16]{1,0:T(8,128)(2,1)} %bitcast.8, bf16[256,256]{1,0:T(8,128)(2,1)} %bitcast.7), custom_call_target="tpu_custom_call" | custom-call | tf_op jit(solution)/shard_map/pallas_call | solution.py:261
  1.7 5.2 %collective-permute-start.2 = (bf16[1,16,128]{2,1,0:T(8,128)(2,1)S(1)}, bf16[1,16,128]{2,1,0:T(8,128)(2,1)S(1)}, u32[]{:S(2)}, u32[]{:S(2)}) collective-permute-start(bf16[1,16,128]{2,1,0:T(8,128)(2,1)S(1)} %get-tuple-element.17), channel_id=1, source_target_pairs={{0,3},{1,2},{2,1},{3,0},{4,7},{5,6},{6,5},{7,4},{8,11},{9,10},{10,... | collective-permute-start | bytes 12296 | tf_op jit(solution)/shard_map/ppermute | solution.py:284
  7.0 0.0 collective-permute-start.1
  7.0 0.4 collective-permute-start
  7.4 2.4 %collective-permute-done = bf16[1,16,128]{2,1,0:T(8,128)(2,1)S(1)} collective-permute-done((bf16[1,16,128]{2,1,0:T(8,128)(2,1)S(1)}, bf16[1,16,128]{2,1,0:T(8,128)(2,1)S(1)}, u32[]{:S(2)}, u32[]{:S(2)}) %collective-permute-start) | collective-permute-done | bytes 4128 | tf_op jit(solution)/shard_map/ppermute | solution.py:284
  9.8 0.6 %collective-permute-done.1 = bf16[1,16,128]{2,1,0:T(8,128)(2,1)S(1)} collective-permute-done((bf16[1,16,128]{2,1,0:T(8,128)(2,1)S(1)}, bf16[1,16,128]{2,1,0:T(8,128)(2,1)S(1)}, u32[]{:S(2)}, u32[]{:S(2)}) %collective-permute-start.1) | collective-permute-done | bytes 4128 | tf_op jit(solution)/shard_map/ppermute | solution.py:284
  10.4 0.0 collective-permute-done.2
  10.4 4.0 %collective-permute-start.3 = (bf16[4,16,128]{2,1,0:T(8,128)(2,1)S(1)}, bf16[4,16,128]{2,1,0:T(8,128)(2,1)S(1)}, u32[]{:S(2)}, u32[]{:S(2)}) collective-permute-start(bf16[4,16,128]{2,1,0:T(8,128)(2,1)S(1)} %constant_dynamic-update-slice_fusion.refs_0_), channel_id=1, source_target_pairs={{0,6},{1,7},{2,4},{3,5},{4,2},{5,3},{6,0},{7,1},{8,14},{9,15},{10,... | collective-permute-start | bytes 49160 | tf_op jit(solution)/shard_map/ppermute | solution.py:284
  14.4 9.5 %all-to-all-start = ((s32[32,1,128]{2,1,0:T(1,128)}), s32[32,1,128]{2,1,0:T(1,128)S(1)}, u32[]{:S(2)}, u32[]{:S(2)}) async-start(s32[32,1,128]{2,1,0:T(1,128)} %bitcast.3), calls=%async_computation | async-start | bytes 32768 | tf_op jit(solution)/shard_map/all_to_all | solution.py:327
  23.8 1.9 %shard_map.38.refs_1_ = f32[3,288,256]{2,1,0:T(8,128)S(1)} custom-call(bf16[256,256]{1,0:T(8,128)(2,1)S(1)} %get-tuple-element.16.coeffs_ref, bf16[4,16,128]{2,1,0:T(8,128)(2,1)S(1)} %constant_dynamic-update-slice_fusion.refs_0_), custom_call_target="tpu_custom_call" | custom-call | tf_op jit(solution)/shard_map/pallas_call | solution.py:261
  25.7 0.0 collective-permute-done.3.refs_0_
  25.8 0.0 copy-start
  25.8 1.9 %shard_map.39 = (bf16[432,512]{1,0:T(8,128)(2,1)S(1)}, bf16[432,512]{1,0:T(8,128)(2,1)S(1)}) custom-call(bf16[256,256]{1,0:T(8,128)(2,1)S(1)} %get-tuple-element.16.coeffs_ref, bf16[4,16,128]{2,1,0:T(8,128)(2,1)S(1)} %collective-permute-done.3.refs_0_, f32[3,288,256]{2,1,0:T(8,128)S(1)} %shard_map.38.refs_1_), custom_call_target="tpu_custom_call" | custom-call | tf_op jit(solution)/shard_map/pallas_call | solution.py:261
  27.7 3.0 %all-to-all-done = s32[32,1,128]{2,1,0:T(1,128)S(1)} async-done(((s32[32,1,128]{2,1,0:T(1,128)}), s32[32,1,128]{2,1,0:T(1,128)S(1)}, u32[]{:S(2)}, u32[]{:S(2)}) %all-to-all-start) | async-done | bytes 16416 | tf_op jit(solution)/shard_map/all_to_all | solution.py:327
  30.7 0.0 copy-done
  30.7 0.7 %shard_map.40 = (bf16[32,16,128]{2,1,0:T(8,128)(2,1)S(1)}, f32[64,128]{1,0:T(8,128)S(1)}, bf16[64,512]{1,0:T(8,128)(2,1)S(1)}) custom-call(s32[32,128]{1,0:T(8,128)S(1)} %get-tuple-element.14.keys_ref, s32[32,128]{1,0:T(8,128)S(1)} %bitcast.6, s32[16,13]{1,0:T(8,128)S(1)} %copy-done, bf16[432,512]{1,0:T(8,128)(2,1)S(1)} %get-tuple-element.18.high_ref, ...), custom_call_target="tpu_custom_call" | custom-call | tf_op jit(solution)/shard_map/pallas_call | solution.py:261
  31.4 10.2 %all_to_all.16.arrived_ref = bf16[32,16,128]{2,1,0:T(8,128)(2,1)S(1)} all-to-all(bf16[32,16,128]{2,1,0:T(8,128)(2,1)S(1)} %get-tuple-element.22), channel_id=1, replica_groups={{160,168,176,184,128,136,144,152,224,232,240,248,192,200,208,216,32,40,..., dimensions={0} | all-to-all | bytes 262144 | tf_op jit(solution)/shard_map/all_to_all | solution.py:347
  41.6 0.8 %shard_map.41 = f32[2,16,256]{2,1,0:T(8,128)} custom-call(f32[64,128]{1,0:T(8,128)S(1)} %get-tuple-element.20.local_ref, bf16[64,512]{1,0:T(8,128)(2,1)S(1)} %get-tuple-element.21.place_ref, bf16[32,16,128]{2,1,0:T(8,128)(2,1)S(1)} %all_to_all.16.arrived_ref), custom_call_target="tpu_custom_call" | custom-call | tf_op jit(solution)/shard_map/pallas_call | solution.py:261
  (4 shorter events, 0.0 us)
Async XLA Ops:
  1.7 8.6 %collective-permute-start.2 = (bf16[1,16,128]{2,1,0:T(8,128)(2,1)S(1)}, bf16[1,16,128]{2,1,0:T(8,128)(2,1)S(1)}, u32[]{:S(2)}, u32[]{:S(2)}) collective-permute-start(bf16[1,16,128]{2,1,0:T(8,128)(2,1)S(1)} %get-tuple-element.17), channel_id=1, source_target_pairs={{0,3},{1,2},{2,1},{3,0},{4,7},{5,6},{6,5},{7,4},{8,11},{9,10},{10,... | collective-permute-start | bytes 12296 | tf_op jit(solution)/shard_map/ppermute | solution.py:284
  7.0 3.4 %collective-permute-start.1 = (bf16[1,16,128]{2,1,0:T(8,128)(2,1)S(1)}, bf16[1,16,128]{2,1,0:T(8,128)(2,1)S(1)}, u32[]{:S(2)}, u32[]{:S(2)}) collective-permute-start(bf16[1,16,128]{2,1,0:T(8,128)(2,1)S(1)} %get-tuple-element.17), channel_id=1, source_target_pairs={{0,2},{1,3},{2,0},{3,1},{4,6},{5,7},{6,4},{7,5},{8,10},{9,11},{10,... | collective-permute-start | bytes 12296 | tf_op jit(solution)/shard_map/ppermute | solution.py:284
  7.0 2.8 %collective-permute-start = (bf16[1,16,128]{2,1,0:T(8,128)(2,1)S(1)}, bf16[1,16,128]{2,1,0:T(8,128)(2,1)S(1)}, u32[]{:S(2)}, u32[]{:S(2)}) collective-permute-start(bf16[1,16,128]{2,1,0:T(8,128)(2,1)S(1)} %get-tuple-element.17), channel_id=1, source_target_pairs={{0,1},{1,0},{2,3},{3,2},{4,5},{5,4},{6,7},{7,6},{8,9},{9,8},{10,11... | collective-permute-start | bytes 12296 | tf_op jit(solution)/shard_map/ppermute | solution.py:284
  10.4 15.4 %collective-permute-start.3 = (bf16[4,16,128]{2,1,0:T(8,128)(2,1)S(1)}, bf16[4,16,128]{2,1,0:T(8,128)(2,1)S(1)}, u32[]{:S(2)}, u32[]{:S(2)}) collective-permute-start(bf16[4,16,128]{2,1,0:T(8,128)(2,1)S(1)} %constant_dynamic-update-slice_fusion.refs_0_), channel_id=1, source_target_pairs={{0,6},{1,7},{2,4},{3,5},{4,2},{5,3},{6,0},{7,1},{8,14},{9,15},{10,... | collective-permute-start | bytes 49160 | tf_op jit(solution)/shard_map/ppermute | solution.py:284
  14.4 16.4 %all-to-all-start = ((s32[32,1,128]{2,1,0:T(1,128)}), s32[32,1,128]{2,1,0:T(1,128)S(1)}, u32[]{:S(2)}, u32[]{:S(2)}) async-start(s32[32,1,128]{2,1,0:T(1,128)} %bitcast.3), calls=%async_computation | async-start | bytes 32768 | tf_op jit(solution)/shard_map/all_to_all | solution.py:327
  25.8 5.0 %copy-start = (s32[16,13]{1,0:T(8,128)S(1)}, s32[16,13]{1,0:T(8,128)}, u32[]{:S(2)}) copy-start(s32[16,13]{1,0:T(8,128)} %neighbors_ref.1) | copy-start | bytes 2500

commit v6 on v5

--- a/solution.py
+++ b/solution.py
@@ -169,17 +169,7 @@
     )
 
 
-def message_kernel(
-    keys_ref,
-    guests_ref,
-    neighbors_ref,
-    high_ref,
-    low_ref,
-    message_ref,
-    local_ref,
-    place_ref,
-    chunk_ref,
-):
+def select_kernel(keys_ref, guests_ref, neighbors_ref, picks_ref, mask_ref, place_ref):
     keys = flipped(keys_ref[...])
     guests = flipped(guests_ref[...])
     spots = []
@@ -195,13 +185,7 @@
     picks = jnp.concatenate(
         [jnp.where(lane == spot, 1.0, 0.0).astype(jnp.bfloat16) for spot in spots], axis=0
     )
-    picked = jnp.dot(picks, high_ref[...], preferred_element_type=jnp.float32)
-    for slot in range(2 * CAP):
-        for part in range(4):
-            chunk_ref[:, 4 * part + slot, :] = picked[
-                32 * slot : 32 * (slot + 1), 128 * part : 128 * (part + 1)
-            ]
-    message_ref[...] = chunk_ref[...].astype(jnp.bfloat16)
+    picks_ref[...] = picks
     myself = lax.axis_index("box").astype(jnp.int32)
     named = neighbors_ref[...]
     within = named - 16 * myself
@@ -220,11 +204,7 @@
     push_mask = jnp.where(jnp.broadcast_to(push, row.shape) == row, 1.0, 0.0)
     same_mask = jnp.where(iota((16, 16), 0) == iota((16, 16), 1), 1.0, 0.0)
     mask = jnp.concatenate([push_mask, same_mask, pull_mask], axis=1).astype(jnp.bfloat16)
-    local = jnp.dot(mask, high_ref[...], preferred_element_type=jnp.float32) + jnp.dot(
-        mask, low_ref[...], preferred_element_type=jnp.float32
-    )
-    for part in range(4):
-        local_ref[16 * part : 16 * (part + 1), :] = local[:, 128 * part : 128 * (part + 1)]
+    mask_ref[...] = mask
     lane = iota((32, 128), 1)
     keys = jnp.where((lane == 2) | (lane == 3), jnp.roll(keys, 2, axis=1), -1)
     target = jnp.where(lane < 2, guests & 15, (keys >> 4) & 15)
@@ -246,6 +226,22 @@
     place_ref[...] = jnp.where(place, 1.0, 0.0).astype(jnp.bfloat16)
 
 
+def message_kernel(picks_ref, mask_ref, high_ref, low_ref, message_ref, local_ref, chunk_ref):
+    picked = jnp.dot(picks_ref[...], high_ref[...], preferred_element_type=jnp.float32)
+    for slot in range(2 * CAP):
+        for part in range(4):
+            chunk_ref[:, 4 * part + slot, :] = picked[
+                32 * slot : 32 * (slot + 1), 128 * part : 128 * (part + 1)
+            ]
+    message_ref[...] = chunk_ref[...].astype(jnp.bfloat16)
+    mask = mask_ref[...]
+    local = jnp.dot(mask, high_ref[...], preferred_element_type=jnp.float32) + jnp.dot(
+        mask, low_ref[...], preferred_element_type=jnp.float32
+    )
+    for part in range(4):
+        local_ref[16 * part : 16 * (part + 1), :] = local[:, 128 * part : 128 * (part + 1)]
+
+
 def gather_kernel(local_ref, place_ref, arrived_ref, out_ref):
     total = local_ref[...] + jnp.dot(
         place_ref[...], arrived_ref[...].reshape(512, 128), preferred_element_type=jnp.float32
@@ -328,18 +324,25 @@
     quad = jnp.concatenate(pieces, axis=0)
     rest = swap(quad, lambda i: i ^ 6)
     total = images([quad], None, False)
-    high, low = images([rest], total, True)
-    message, local, place = call(
-        message_kernel,
+    picks, mask, place = call(
+        select_kernel,
         (
-            shape((groups, 16, 128), jnp.bfloat16),
-            shape((64, 128), jnp.float32),
+            shape((2 * CAP * groups, 27 * box_count), jnp.bfloat16),
+            shape((box_count, 27 * box_count), jnp.bfloat16),
             shape((64, 16 * groups), jnp.bfloat16),
         ),
-        [pltpu.VMEM((groups, 16, 128), jnp.float32)],
+        [],
         near(own),
         near(guests),
         near(neighbors),
+    )
+    high, low = images([rest], total, True)
+    message, local = call(
+        message_kernel,
+        (shape((groups, 16, 128), jnp.bfloat16), shape((64, 128), jnp.float32)),
+        [pltpu.VMEM((groups, 16, 128), jnp.float32)],
+        near(picks),
+        near(mask),
         near(high),
         near(low),
     )

time: 42.6 us -> 43.6 us (1.023)
  waiting for transfers between devices: 5.98 us -> 9.19 us
  starting transfers between devices: 19.1 us -> 16.8 us
    ppermute x4, starting transfers between devices: 9.63 us -> 7.04 us  [swap(): lax.ppermute(value, 'term', [(i, other(i) % terms) for i in range(terms)])]
    all_to_all x1, waiting for transfers between devices: 3.01 us -> 4.96 us  [on_device(): lax.all_to_all(keys, 'box', split_axis=0, concat_axis=0, tiled=True)]
    ppermute x4, waiting for transfers between devices: 2.97 us -> 4.23 us  [swap(): lax.ppermute(value, 'term', [(i, other(i) % terms) for i in range(terms)])]
    pallas_call x5 -> x6, Pallas kernels: 7.07 us -> 7 us  [call(): pl.pallas_call(kernel, out_shape=outs, in_specs=[pl.BlockSpec(memory_spac...]
  transfers between devices with their start and end apart: 5 -> 5, of which waited for: 3 -> 3; matrix products, arithmetic and copies ran while one was open for 0% -> 0% of each run, Pallas kernels for 9% -> 5%
where the time goes in v6:
time: 43.6 us; the launch traced here: 43.3 us
  starting transfers between devices  16.8 us (39%)
  blocking collectives  10.2 us (23%)
  waiting for transfers between devices  9.19 us (21%)
  Pallas kernels  7 us (16%)
    all_to_all x1, blocking collectives, on_device(): lax.all_to_all(message, 'box', split_axis=0, concat_axis=0, tiled=True, a...  10.2 us
    all_to_all x1, starting transfers between devices, on_device(): lax.all_to_all(keys, 'box', split_axis=0, concat_axis=0, tiled=True)  9.75 us
    ppermute x4, starting transfers between devices, swap(): lax.ppermute(value, 'term', [(i, other(i) % terms) for i in range(terms)])  7.04 us
    pallas_call x6, Pallas kernels, call(): pl.pallas_call(kernel, out_shape=outs, in_specs=[pl.BlockSpec(memory_spac...  7 us
    all_to_all x1, waiting for transfers between devices, on_device(): lax.all_to_all(keys, 'box', split_axis=0, concat_axis=0, tiled=True)  4.96 us
    ppermute x4, waiting for transfers between devices, swap(): lax.ppermute(value, 'term', [(i, other(i) % terms) for i in range(terms)])  4.23 us
  transfers between devices with their start and end apart: 5, of which 3 were waited for; matrix products, arithmetic and copies ran while one was open for 0% of the time, Pallas kernels for 5%

profile of v6, /device:TPU:1, one launch (start us, length us, event | category | flops | bytes accessed | tf_op | source)
XLA Modules:
  0.0 43.3 jit_solution(17490146035183148964)
XLA Ops:
  0.0 1.7 %shard_map.37 = (s32[32,128]{1,0:T(8,128)}, s32[32,128]{1,0:T(8,128)S(1)}, bf16[1,16,128]{2,1,0:T(8,128)(2,1)S(1)}, bf16[256,256]{1,0:T(8,128)(2,1)S(1)}) custom-call(s32[16,13]{1,0:T(8,128)} %neighbors_ref.1, bf16[96,16]{1,0:T(8,128)(2,1)} %bitcast.8, bf16[256,256]{1,0:T(8,128)(2,1)} %bitcast.7), custom_call_target="tpu_custom_call" | custom-call | tf_op jit(solution)/shard_map/pallas_call | solution.py:257
  1.7 2.5 %collective-permute-start = (bf16[1,16,128]{2,1,0:T(8,128)(2,1)S(1)}, bf16[1,16,128]{2,1,0:T(8,128)(2,1)S(1)}, u32[]{:S(2)}, u32[]{:S(2)}) collective-permute-start(bf16[1,16,128]{2,1,0:T(8,128)(2,1)S(1)} %get-tuple-element.21), channel_id=1, source_target_pairs={{0,1},{1,0},{2,3},{3,2},{4,5},{5,4},{6,7},{7,6},{8,9},{9,8},{10,11... | collective-permute-start | bytes 12296 | tf_op jit(solution)/shard_map/ppermute | solution.py:280
  4.3 3.0 %collective-permute-start.1 = (bf16[1,16,128]{2,1,0:T(8,128)(2,1)S(1)}, bf16[1,16,128]{2,1,0:T(8,128)(2,1)S(1)}, u32[]{:S(2)}, u32[]{:S(2)}) collective-permute-start(bf16[1,16,128]{2,1,0:T(8,128)(2,1)S(1)} %get-tuple-element.21), channel_id=1, source_target_pairs={{0,2},{1,3},{2,0},{3,1},{4,6},{5,7},{6,4},{7,5},{8,10},{9,11},{10,... | collective-permute-start | bytes 12296 | tf_op jit(solution)/shard_map/ppermute | solution.py:280
  7.3 0.0 collective-permute-start.2
  7.3 0.0 collective-permute-done
  7.3 1.0 %collective-permute-done.1 = bf16[1,16,128]{2,1,0:T(8,128)(2,1)S(1)} collective-permute-done((bf16[1,16,128]{2,1,0:T(8,128)(2,1)S(1)}, bf16[1,16,128]{2,1,0:T(8,128)(2,1)S(1)}, u32[]{:S(2)}, u32[]{:S(2)}) %collective-permute-start.1) | collective-permute-done | bytes 4128 | tf_op jit(solution)/shard_map/ppermute | solution.py:280
  8.3 3.3 %collective-permute-done.2 = bf16[1,16,128]{2,1,0:T(8,128)(2,1)S(1)} collective-permute-done((bf16[1,16,128]{2,1,0:T(8,128)(2,1)S(1)}, bf16[1,16,128]{2,1,0:T(8,128)(2,1)S(1)}, u32[]{:S(2)}, u32[]{:S(2)}) %collective-permute-start.2) | collective-permute-done | bytes 4128 | tf_op jit(solution)/shard_map/ppermute | solution.py:280
  11.5 1.5 %collective-permute-start.3 = (bf16[4,16,128]{2,1,0:T(8,128)(2,1)S(1)}, bf16[4,16,128]{2,1,0:T(8,128)(2,1)S(1)}, u32[]{:S(2)}, u32[]{:S(2)}) collective-permute-start(bf16[4,16,128]{2,1,0:T(8,128)(2,1)S(1)} %constant_dynamic-update-slice_fusion.refs_0_), channel_id=1, source_target_pairs={{0,6},{1,7},{2,4},{3,5},{4,2},{5,3},{6,0},{7,1},{8,14},{9,15},{10,... | collective-permute-start | bytes 49160 | tf_op jit(solution)/shard_map/ppermute | solution.py:280
  13.0 9.7 %all-to-all-start = ((s32[32,1,128]{2,1,0:T(1,128)}), s32[32,1,128]{2,1,0:T(1,128)S(1)}, u32[]{:S(2)}, u32[]{:S(2)}) async-start(s32[32,1,128]{2,1,0:T(1,128)} %bitcast.3), calls=%async_computation | async-start | bytes 32768 | tf_op jit(solution)/shard_map/all_to_all | solution.py:323
  22.8 0.0 copy-start
  22.8 1.9 %shard_map.39.refs_1_ = f32[3,288,256]{2,1,0:T(8,128)S(1)} custom-call(bf16[256,256]{1,0:T(8,128)(2,1)S(1)} %get-tuple-element.20.coeffs_ref, bf16[4,16,128]{2,1,0:T(8,128)(2,1)S(1)} %constant_dynamic-update-slice_fusion.refs_0_), custom_call_target="tpu_custom_call" | custom-call | tf_op jit(solution)/shard_map/pallas_call | solution.py:257
  24.7 5.0 %all-to-all-done = s32[32,1,128]{2,1,0:T(1,128)S(1)} async-done(((s32[32,1,128]{2,1,0:T(1,128)}), s32[32,1,128]{2,1,0:T(1,128)S(1)}, u32[]{:S(2)}, u32[]{:S(2)}) %all-to-all-start) | async-done | bytes 16416 | tf_op jit(solution)/shard_map/all_to_all | solution.py:323
  29.7 0.0 copy-done
  29.7 0.3 shard_map.38
  30.0 0.0 collective-permute-done.3.refs_0_
  30.0 1.9 %shard_map.40 = (bf16[432,512]{1,0:T(8,128)(2,1)S(1)}, bf16[432,512]{1,0:T(8,128)(2,1)S(1)}) custom-call(bf16[256,256]{1,0:T(8,128)(2,1)S(1)} %get-tuple-element.20.coeffs_ref, bf16[4,16,128]{2,1,0:T(8,128)(2,1)S(1)} %collective-permute-done.3.refs_0_, f32[3,288,256]{2,1,0:T(8,128)S(1)} %shard_map.39.refs_1_), custom_call_target="tpu_custom_call" | custom-call | tf_op jit(solution)/shard_map/pallas_call | solution.py:257
  31.9 0.4 shard_map.41
  32.3 10.2 %all_to_all.16.arrived_ref = bf16[32,16,128]{2,1,0:T(8,128)(2,1)S(1)} all-to-all(bf16[32,16,128]{2,1,0:T(8,128)(2,1)S(1)} %get-tuple-element.26), channel_id=1, replica_groups={{160,168,176,184,128,136,144,152,224,232,240,248,192,200,208,216,32,40,..., dimensions={0} | all-to-all | bytes 262144 | tf_op jit(solution)/shard_map/all_to_all | solution.py:350
  42.5 0.8 %shard_map.42 = f32[2,16,256]{2,1,0:T(8,128)} custom-call(f32[64,128]{1,0:T(8,128)S(1)} %get-tuple-element.24.local_ref, bf16[64,512]{1,0:T(8,128)(2,1)S(1)} %get-tuple-element.25.place_ref, bf16[32,16,128]{2,1,0:T(8,128)(2,1)S(1)} %all_to_all.16.arrived_ref), custom_call_target="tpu_custom_call" | custom-call | tf_op jit(solution)/shard_map/pallas_call | solution.py:257
  (4 shorter events, 0.0 us)
Async XLA Ops:
  1.7 5.5 %collective-permute-start = (bf16[1,16,128]{2,1,0:T(8,128)(2,1)S(1)}, bf16[1,16,128]{2,1,0:T(8,128)(2,1)S(1)}, u32[]{:S(2)}, u32[]{:S(2)}) collective-permute-start(bf16[1,16,128]{2,1,0:T(8,128)(2,1)S(1)} %get-tuple-element.21), channel_id=1, source_target_pairs={{0,1},{1,0},{2,3},{3,2},{4,5},{5,4},{6,7},{7,6},{8,9},{9,8},{10,11... | collective-permute-start | bytes 12296 | tf_op jit(solution)/shard_map/ppermute | solution.py:280
  4.3 4.0 %collective-permute-start.1 = (bf16[1,16,128]{2,1,0:T(8,128)(2,1)S(1)}, bf16[1,16,128]{2,1,0:T(8,128)(2,1)S(1)}, u32[]{:S(2)}, u32[]{:S(2)}) collective-permute-start(bf16[1,16,128]{2,1,0:T(8,128)(2,1)S(1)} %get-tuple-element.21), channel_id=1, source_target_pairs={{0,2},{1,3},{2,0},{3,1},{4,6},{5,7},{6,4},{7,5},{8,10},{9,11},{10,... | collective-permute-start | bytes 12296 | tf_op jit(solution)/shard_map/ppermute | solution.py:280
  7.3 4.3 %collective-permute-start.2 = (bf16[1,16,128]{2,1,0:T(8,128)(2,1)S(1)}, bf16[1,16,128]{2,1,0:T(8,128)(2,1)S(1)}, u32[]{:S(2)}, u32[]{:S(2)}) collective-permute-start(bf16[1,16,128]{2,1,0:T(8,128)(2,1)S(1)} %get-tuple-element.21), channel_id=1, source_target_pairs={{0,3},{1,2},{2,1},{3,0},{4,7},{5,6},{6,5},{7,4},{8,11},{9,10},{10,... | collective-permute-start | bytes 12296 | tf_op jit(solution)/shard_map/ppermute | solution.py:280
  11.5 18.4 %collective-permute-start.3 = (bf16[4,16,128]{2,1,0:T(8,128)(2,1)S(1)}, bf16[4,16,128]{2,1,0:T(8,128)(2,1)S(1)}, u32[]{:S(2)}, u32[]{:S(2)}) collective-permute-start(bf16[4,16,128]{2,1,0:T(8,128)(2,1)S(1)} %constant_dynamic-update-slice_fusion.refs_0_), channel_id=1, source_target_pairs={{0,6},{1,7},{2,4},{3,5},{4,2},{5,3},{6,0},{7,1},{8,14},{9,15},{10,... | collective-permute-start | bytes 49160 | tf_op jit(solution)/shard_map/ppermute | solution.py:280
  13.0 16.6 %all-to-all-start = ((s32[32,1,128]{2,1,0:T(1,128)}), s32[32,1,128]{2,1,0:T(1,128)S(1)}, u32[]{:S(2)}, u32[]{:S(2)}) async-start(s32[32,1,128]{2,1,0:T(1,128)} %bitcast.3), calls=%async_computation | async-start | bytes 32768 | tf_op jit(solution)/shard_map/all_to_all | solution.py:323
  22.8 6.9 %copy-start = (s32[16,13]{1,0:T(8,128)S(1)}, s32[16,13]{1,0:T(8,128)}, u32[]{:S(2)}) copy-start(s32[16,13]{1,0:T(8,128)} %neighbors_ref.1) | copy-start | bytes 2500
